TPU v7x, 128 devices: a whole 4x4x4 slice. The times are simulated.
128 devices in a mesh: seq: 64 (over y, z, x), ch: 2 (over core).
Axes of the slice: x: 4, y: 4, z: 4, core: 2. Of those that a mesh axis runs over, the one named last changes fastest.
Arguments:
- cotangent: bfloat16 [16384, 2, 2048], P('seq', None, 'ch'), may hold values from -6 to 6
- conv_input: bfloat16 [16384, 2, 2048], P('seq', None, 'ch'), may hold values from -6 to 6
- decay_rate: bfloat16 [16384, 2048], P('seq', 'ch'), may hold values from 2.4414063e-06 to 0.7
- angle: float32 [2048], P('ch'), may hold values from -3.140625 to 3.140625
- conv_weight: float32 [4, 2, 2048], P(None, None, 'ch'), may hold values from -3 to 3
- in_weight: bfloat16 [4096, 2, 2048], P(None, None, 'ch'), may hold values from -0.09375 to 0.09375
Outputs:
- input_grad: bfloat16 [16384, 4096], P(('seq', 'ch'))
- channel_major: bfloat16 [2, 2048, 16384], P(None, ('ch', 'seq'))
- tap_grad: float32 [4, 2, 2048], P(None, None, 'ch')
All inputs are finite; a program needn't handle non-finite values.
Results may differ from a plain program's by a relative error of at most 0.0085.
Values may be sent and summed in bfloat16 or wider, within the bound.
A program may use at most 128 MiB of HBM per device.

v0:
```python
import jax
import jax.numpy as jnp
from jax import lax
from jax.sharding import PartitionSpec as P


def prefix(value, axis, join, neutral):
    count, mine = (lax.axis_size(axis), lax.axis_index(axis))
    pieces = jax.tree.map(lambda part: lax.all_gather(part, axis), value)
    pieces = jax.tree.map(lambda part: part[::-1], pieces)
    mine = count - 1 - mine
    total = jax.tree.map(
        lambda part, zero: jnp.full_like(part, 0) + jnp.asarray(zero, part.dtype), value, neutral
    )

    def hop(position, total):
        longer = join(total, jax.tree.map(lambda part: part[position], pieces))
        return jax.tree.map(lambda new, old: jnp.where(position < mine, new, old), longer, total)

    return lax.fori_loop(0, count - 1, hop, total)


def passed_along(array, axis, by):
    count = lax.axis_size(axis)
    pairs = [(i, i + by) for i in range(count) if 0 <= i + by < count]
    return lax.ppermute(array, axis, pairs)


def compose(earlier, later):
    outer_real, outer_imag, outer_shift_real, outer_shift_imag = earlier
    inner_real, inner_imag, inner_shift_real, inner_shift_imag = later
    return (
        inner_real * outer_real - inner_imag * outer_imag,
        inner_real * outer_imag + inner_imag * outer_real,
        inner_real * outer_shift_real - inner_imag * outer_shift_imag + inner_shift_real,
        inner_real * outer_shift_imag + inner_imag * outer_shift_real + inner_shift_imag,
    )


def local_block(cotangent, decay_rate, angle):
    rates = decay_rate.astype(jnp.float32)
    modulus = jnp.exp(-rates)
    mult_real = modulus * jnp.cos(angle)[None, :]
    mult_imag = -modulus * jnp.sin(angle)[None, :]
    step_real = jnp.concatenate([mult_real[1:], jnp.ones_like(mult_real[:1])], 0)
    step_imag = jnp.concatenate([mult_imag[1:], jnp.zeros_like(mult_imag[:1])], 0)
    upstream = cotangent.astype(jnp.float32)
    elements = (step_real[::-1], step_imag[::-1], upstream[::-1, 0], upstream[::-1, 1])
    scanned = lax.associative_scan(compose, elements, axis=0)
    prod_real, prod_imag, base_real, base_imag = [member[::-1] for member in scanned]
    return (rates, mult_real, mult_imag, prod_real, prod_imag, base_real, base_imag)


def on_device(cotangent, conv_input, decay_rate, angle, conv_weight, in_weight):
    rates, mult_real, mult_imag, prod_real, prod_imag, base_real, base_imag = local_block(
        cotangent, decay_rate, angle
    )
    length = cotangent.shape[0]
    width = cotangent.shape[2]
    map_real = mult_real[0] * prod_real[0] - mult_imag[0] * prod_imag[0]
    map_imag = mult_real[0] * prod_imag[0] + mult_imag[0] * prod_real[0]
    shift_real = mult_real[0] * base_real[0] - mult_imag[0] * base_imag[0]
    shift_imag = mult_real[0] * base_imag[0] + mult_imag[0] * base_real[0]
    ones_vec = jnp.ones((width,), jnp.float32)
    zero_vec = jnp.zeros((width,), jnp.float32)
    carried = prefix(
        (map_real, map_imag, shift_real, shift_imag),
        "seq",
        compose,
        (ones_vec, zero_vec, zero_vec, zero_vec),
    )
    carry_real = carried[2]
    carry_imag = carried[3]
    grad_real = base_real + prod_real * carry_real[None] - prod_imag * carry_imag[None]
    grad_imag = base_imag + prod_real * carry_imag[None] + prod_imag * carry_real[None]
    scaling = jnp.sqrt(-jnp.expm1(-2.0 * rates))
    conv_grad = jnp.stack([grad_real * scaling, grad_imag * scaling], 1)
    upper_rim = passed_along(conv_grad[:3], "seq", -1)
    extended = jnp.concatenate([conv_grad, upper_rim], 0)
    feature_sum = conv_weight[0][None] * extended[0:length]
    for tap_index in range(1, 4):
        feature_sum = (
            feature_sum + conv_weight[tap_index][None] * extended[tap_index : tap_index + length]
        )
    input_feat = feature_sum.astype(jnp.bfloat16)
    lower_rim = passed_along(conv_input[length - 3 :], "seq", 1)
    shifted_input = jnp.concatenate([lower_rim, conv_input], 0).astype(jnp.float32)
    taps = []
    for tap_index in range(4):
        taps.append(
            jnp.sum(conv_grad * shifted_input[3 - tap_index : 3 - tap_index + length], axis=0)
        )
    tap_grad = lax.psum(jnp.stack(taps, 0), "seq")
    layout = jnp.transpose(input_feat, (1, 2, 0))
    channel_major = lax.all_to_all(layout, "seq", split_axis=1, concat_axis=2, tiled=True)
    summed = lax.psum_scatter(
        lax.dot_general(
            input_feat, in_weight, (((1, 2), (1, 2)), ((), ())), preferred_element_type=jnp.float32
        ).astype(jnp.bfloat16),
        "ch",
        scatter_dimension=0,
        tiled=True,
    )
    return (summed, channel_major, tap_grad)


def solution(mesh):
    in_specs = (
        P("seq", None, "ch"),
        P("seq", None, "ch"),
        P("seq", "ch"),
        P("ch"),
        P(None, None, "ch"),
        P(None, None, "ch"),
    )
    out_specs = (P(("seq", "ch"), None), P(None, ("ch", "seq"), None), P(None, None, "ch"))
    return jax.shard_map(
        on_device, mesh=mesh, in_specs=in_specs, out_specs=out_specs, check_vma=False
    )
```

profile of v0, /device:TPU:0, one launch (start us, length us, event | category | flops | bytes accessed | tf_op | source)
XLA Modules:
  0.0 1332.5 jit_solution(1409491636093875351)
XLA Ops:
  8.5 4.1 collective-permute-start.1
  33.6 2.7 slice.587
  36.2 2.7 slice.576
  38.9 2.6 slice.581
  41.5 2.7 slice.589
  44.2 2.3 add_add_fusion.1
  86.9 2.1 pad.229
  89.0 4.6 pad.263
  93.6 2.3 add.579
  99.1 2.1 pad.261
  103.1 4.6 pad.260
  107.7 2.3 add.575
  111.9 8.9 rev.34
  120.9 5.2 rev.41
  126.1 176.5 %all-gather.3 = f32[64,1,1024]{2,1,0:T(1,128)S(1)} all-gather(f32[1,1,1024]{2,1,0:T(1,128)S(1)} %get-tuple-element.198), channel_id=1, replica_groups=mesh['seq'=64,'ch'=2] {'seq'}, dimensions={0}, use_global_device_ids=true | all-gather | bytes 266240 | tf_op jit(solution)/shard_map/all_gather | solution.py:9
  302.7 2.6 rev.39
  305.3 170.6 %all-gather.2 = f32[64,1,1024]{2,1,0:T(1,128)S(1)} all-gather(f32[1,1,1024]{2,1,0:T(1,128)S(1)} %get-tuple-element.199), channel_id=1, replica_groups=mesh['seq'=64,'ch'=2] {'seq'}, dimensions={0}, use_global_device_ids=true | all-gather | bytes 266240 | tf_op jit(solution)/shard_map/all_gather | solution.py:9
  476.0 2.5 rev.38
  479.1 5.2 rev.40
  484.3 172.6 %all-gather.1 = f32[64,1,1024]{2,1,0:T(1,128)S(1)} all-gather(f32[1,1,1024]{2,1,0:T(1,128)S(1)} %get-tuple-element.200), channel_id=1, replica_groups=mesh['seq'=64,'ch'=2] {'seq'}, dimensions={0}, use_global_device_ids=true | all-gather | bytes 266240 | tf_op jit(solution)/shard_map/all_gather | solution.py:9
  656.9 2.5 rev.37
  659.5 170.6 %all-gather = f32[64,1,1024]{2,1,0:T(1,128)S(1)} all-gather(f32[1,1,1024]{2,1,0:T(1,128)S(1)} %get-tuple-element.201), channel_id=1, replica_groups=mesh['seq'=64,'ch'=2] {'seq'}, dimensions={0}, use_global_device_ids=true | all-gather | bytes 266240 | tf_op jit(solution)/shard_map/all_gather | solution.py:9
  830.1 2.5 rev.36
  832.7 102.7 %while.16 = (s32[]{:T(128)}, f32[1024]{0:T(1024)S(1)}, f32[1024]{0:T(1024)S(1)}, s32[]{:T(128)}, f32[64,1024]{1,0:T(8,128)}, /*index=5*/f32[64,1024]{1,0:T(8,128...) while((s32[]{:T(128)}, f32[1024]{0:T(1024)S(1)}, f32[1024]{0:T(1024)S(1)}, ...), condition=%wide.region_1.2_spmd.clone, body=%wide.region_0.1_spmd.clone.sunk | while | flops 12292 | bytes 65673 | solution.py:20
  935.4 2.4 fusion.23
  942.8 2.6 collective-permute-done
  945.3 1.9 pad_maximum_fusion.1
  947.3 8.0 fusion.11
  955.2 12.7 fusion.5
  967.9 3.1 copy.31
  971.0 4.7 all-to-all-start
  975.7 348.7 %psum.7 = f32[4,2,1024]{2,1,0:T(2,128)} all-reduce(f32[4,2,1024]{2,1,0:T(2,128)S(1)} %pad_maximum_fusion.20), channel_id=1, replica_groups=mesh['seq'=64,'ch'=2] {'seq'}, use_global_device_ids=true, to_apply=%region_7.8 | all-reduce | flops 8192 | bytes 65536 | tf_op jit(solution)/shard_map/psum | solution.py:93
  (542 shorter events, 175.7 us)
Async XLA Ops:
  7.2 1318.5 %reduce-scatter.2.cloned.1.call-start = ((), (), s32[]{:S(2)}) async-start(), calls=%async_computation.2 | async-start | bytes 3145728 | tf_op jit(solution)/shard_map/reduce_scatter | solution.py:96
  8.5 932.4 %collective-permute-start.1 = (bf16[3,2,1024]{2,1,0:T(2,128)(2,1)}, bf16[3,2,1024]{2,1,0:T(2,128)(2,1)}, u32[]{:S(2)}, u32[]{:S(2)}) collective-permute-start(bf16[3,2,1024]{2,1,0:T(2,128)(2,1)} %slice.741), channel_id=1, source_target_pairs={{0,2},{2,4},{4,6},{6,8},{8,10},{10,12},{12,14},{14,16},{16,18},{18... | collective-permute-start | bytes 36872 | tf_op jit(solution)/shard_map/ppermute | solution.py:26
  14.7 5.5 copy-start.5
  20.4 4.4 copy-start.24
  29.1 4.4 copy-start.19
  29.1 7.1 copy-start.18
  33.5 5.3 copy-start.21
  33.6 8.0 copy-start.20
  59.8 2.8 copy-start.40
  61.9 3.3 copy-start.34
  61.9 4.8 copy-start.33
  62.7 4.0 copy-start.35
  62.7 4.0 copy-start.39
  66.8 3.9 copy-start.11
  67.6 4.0 copy-start.25
  67.6 4.0 copy-start.26
  71.6 2.6 copy-start.31
  71.8 4.2 copy-start.30
  71.9 5.8 copy-start.29
  74.2 5.2 copy-start.28
  74.3 5.2 copy-start.27
  79.6 2.6 copy-start
  79.6 2.6 copy-start.2
  110.8 10.1 copy-start.6
  120.9 357.6 %copy-start.8 = (f32[256,1024]{1,0:T(8,128)S(1)}, f32[256,1024]{1,0:T(8,128)}, u32[]{:S(2)}) copy-start(f32[256,1024]{1,0:T(8,128)} %add.573) | copy-start | bytes 3145732
  302.7 176.3 %copy-start.7 = (f32[256,1024]{1,0:T(8,128)S(1)}, f32[256,1024]{1,0:T(8,128)}, u32[]{:S(2)}) copy-start(f32[256,1024]{1,0:T(8,128)} %add.575) | copy-start | bytes 3145732
  484.2 451.1 %copy-start.9 = (f32[256,1024]{1,0:T(8,128)S(1)}, f32[256,1024]{1,0:T(8,128)}, u32[]{:S(2)}) copy-start(f32[256,1024]{1,0:T(8,128)} %rev.34) | copy-start | bytes 3145732
  484.3 451.1 %copy-start.10 = (f32[256,1024]{1,0:T(8,128)S(1)}, f32[256,1024]{1,0:T(8,128)}, u32[]{:S(2)}) copy-start(f32[256,1024]{1,0:T(8,128)} %rev.41) | copy-start | bytes 3145732
  938.5 2.4 copy-start.36
  938.5 2.5 copy-start.23
  939.6 5.7 collective-permute-start
  971.0 353.4 %all-to-all-start = ((bf16[2,1024,256]{2,0,1:T(2,128)(2,1)}), bf16[2,1024,256]{2,0,1:T(2,128)(2,1)S(1)}, u32[]{:S(2)}, u32[]{:S(2)}) async-start(bf16[2,1024,256]{2,0,1:T(2,128)(2,1)} %copy.31), calls=%async_computation.1 | async-start | bytes 2097152 | tf_op jit(solution)/shard_map/all_to_all | solution.py:95
  (15 other events, 19.7 us)
Sparse Core Ops, SparseCore 0:
  968.0 7.8 reduce-scatter.1
where the time goes:
time: 1340 us; the launch traced here: 1330 us
  blocking collectives  1040 us (78%)
  local copies, waits for them, and re-layouts  205 us (15%)
  other arithmetic  44.8 us (3%)
  between operations  15.7 us (1%)
    all_gather x4, blocking collectives, prefix(): pieces = jax.tree.map(lambda part: lax.all_gather(part, axis), value)  690 us
    psum x1, blocking collectives, on_device(): tap_grad = lax.psum(jnp.stack(taps, 0), 'seq')  349 us
    dynamic_slice x126, local copies, waits for them, and re-layouts, hop(): longer = join(total, jax.tree.map(lambda part: part[position], pieces))  99.6 us
    slice x110, local copies, waits for them, and re-layouts, local_block(): scanned = lax.associative_scan(compose, elements, axis=0)  36.3 us
  transfers between devices with their start and end apart: 4, of which 1 were waited for; matrix products, arithmetic and copies ran while one was open for 18% of the time, Pallas kernels for 0%

commit v1 on v0

v1 whole, which is shorter than its diff:
```python
import functools

import jax
import jax.numpy as jnp
from jax import lax
from jax.experimental import pallas as pl
from jax.experimental.pallas import tpu as pltpu
from jax.sharding import PartitionSpec as P

MESH = pl.DeviceIdType.MESH
F32 = jnp.float32
BF16 = jnp.bfloat16
CHUNKS = 8
WCH = 8
EARLY = 8
NT = 8


def cmul(ar, ai, br, bi):
    return ar * br - ai * bi, ar * bi + ai * br


def kernel(
    n_seq, T, C, D,
    cot_h, x_h, dec_h, ang_ref, cw_ref, w_h,
    out_h, cm_h, tap_ref,
    cot_b, x_b, dec_b, w_b, halo_c, halo_d,
    cot_f, x_f, dec_f, e_f, g_f, wtmp, wk, ftmp, feat, featT,
    mapv, maps, part, part_r, obuf, tbuf, trcv, trow,
    in_sem, w_sem, halo_s, halo_r, map_s, map_r, a2a_s, a2a_r, loc_s, par_s, par_r, t1_s, t1_r, t2_s, t2_r, o_sem,
):
    me = lax.axis_index("seq")
    ch = lax.axis_index("ch")
    other = 1 - ch
    NJ = C // 128
    L = T // CHUNKS

    def peer(s):
        return lax.rem(me + s, n_seq)

    barrier = pltpu.get_barrier_semaphore()

    def greet(s, _):
        pl.semaphore_signal(barrier, inc=1, device_id=(peer(s), ch), device_id_type=MESH)
        return 0

    lax.fori_loop(1, n_seq, greet, 0)
    pl.semaphore_signal(barrier, inc=1, device_id=(me, other), device_id_type=MESH)

    c_dec = pltpu.make_async_copy(dec_h, dec_b, in_sem.at[0])
    c_cot = pltpu.make_async_copy(cot_h, cot_b, in_sem.at[1])
    c_x = pltpu.make_async_copy(x_h, x_b, in_sem.at[2])
    c_dec.start()
    c_cot.start()
    c_x.start()
    wrows = w_h.shape[0] // WCH
    for i in range(WCH):
        pltpu.make_async_copy(
            w_h.at[pl.ds(i * wrows, wrows)], w_b.at[pl.ds(i * wrows, wrows)], w_sem.at[i]
        ).start()

    ang = ang_ref[...]
    cr = jnp.cos(ang)
    ci = -jnp.sin(ang)

    def to_f32(src, dst):
        def body(i, _):
            r = pl.multiple_of(i * 64, 64)
            dst[pl.ds(r, 64), :] = src[pl.ds(r, 64), :].astype(F32)
            return 0

        lax.fori_loop(0, src.shape[0] // 64, body, 0)

    def pair(ref, t):
        return ref[pl.ds(2 * NJ * t, NJ, stride=2), :], ref[pl.ds(2 * NJ * t + 1, NJ, stride=2), :]

    c_dec.wait()
    to_f32(dec_b, dec_f)
    c_cot.wait()
    to_f32(cot_b, cot_f)

    zero = jnp.zeros((NJ, 128), F32)

    def pass1(n, st):
        j = L - 1 - n
        out = []
        for c in range(CHUNKS):
            ur, ui, rs = st[3 * c : 3 * c + 3]
            t = c * L + j
            r = dec_f[pl.ds(8 * NJ * (t // 8) + lax.rem(t, 8), NJ, stride=8), :]
            e = jnp.exp(-r)
            e_f[t] = e
            a, b = pair(cot_f, t)
            ur, ui = cmul(e * cr, e * ci, a + ur, b + ui)
            out += [ur, ui, rs + r]
        return tuple(out)

    st = lax.fori_loop(0, L, pass1, (zero,) * (3 * CHUNKS))

    def power(n):
        ar, ai = cr, ci
        while n > 1:
            ar, ai = ar * ar - ai * ai, 2.0 * ar * ai
            n //= 2
        return ar, ai

    lr, li = power(L)
    tr, ti = power(T)
    chunk_maps = []
    for c in range(CHUNKS):
        ur, ui, rs = st[3 * c : 3 * c + 3]
        p = jnp.exp(-rs)
        chunk_maps.append((p * lr, p * li, ur, ui))
    br, bi = zero, zero
    total = zero
    for c in reversed(range(CHUNKS)):
        ar, ai, sr, si = chunk_maps[c]
        br, bi = cmul(ar, ai, br, bi)
        br, bi = br + sr, bi + si
        total = total + st[3 * c + 2]
    mapv[0] = jnp.exp(-total)
    mapv[1] = br
    mapv[2] = bi

    pl.semaphore_wait(barrier, n_seq)

    def map_copy(src_dev, dst_dev):
        return pltpu.make_async_remote_copy(
            src_ref=mapv, dst_ref=maps.at[src_dev], send_sem=map_s.at[dst_dev], recv_sem=map_r.at[src_dev],
            device_id=(dst_dev, ch), device_id_type=MESH)

    def halo_copies(dst_dev):
        return [
            pltpu.make_async_remote_copy(
                src_ref=s, dst_ref=d, send_sem=halo_s.at[i], recv_sem=halo_r.at[i],
                device_id=(dst_dev, ch), device_id_type=MESH)
            for i, (s, d) in enumerate(
                ((cot_b.at[pl.ds(0, 64)], halo_c), (dec_b.at[pl.ds(0, 64)], halo_d)))
        ]

    def send_map(s, _):
        map_copy(me, me - 1 - s).start()
        return 0

    lax.fori_loop(0, me, send_map, 0)

    @pl.when(me > 0)
    def _():
        for c in halo_copies(me - 1):
            c.start()

    def scale_body(t, _):
        r = dec_f[pl.ds(8 * NJ * (t // 8) + lax.rem(t, 8), NJ, stride=8), :]
        g_f[t, 0] = scale_of(r)
        return 0

    def scale_of(r):
        y = 0.25 * r
        q = y * (1.0 - y * (1 / 2) * (1.0 - y * (1 / 3) * (1.0 - y * (1 / 4) * (1.0 - y * (1 / 5) * (1.0 - y * (1 / 6))))))
        q = q * (2.0 - q)
        q = q * (2.0 - q)
        q = q * (2.0 - q)
        return jnp.sqrt(q)

    lax.fori_loop(0, T, scale_body, 0)
    c_x.wait()
    to_f32(x_b, x_f)

    def w_wait(i):
        pltpu.make_async_copy(
            w_h.at[pl.ds(i * wrows, wrows)], w_b.at[pl.ds(i * wrows, wrows)], w_sem.at[i]
        ).wait()

    G = 16 * 2 * NJ

    def unpack_w(i):
        w_wait(i)
        base = i * (wrows // (2 * NJ))

        def body(k, _):
            d0 = pl.multiple_of(base + k * 16, 16)
            slot = lax.rem(k, 2)
            tmp = wtmp.at[slot]
            tmp[...] = w_b[pl.ds(pl.multiple_of(d0 * 2 * NJ, G), G), :].astype(F32)
            for p in range(2):
                for jt in range(NJ):
                    v = tmp[pl.ds(2 * jt + p, 16, stride=2 * NJ), :]
                    wk[pl.ds(d0, 16), pl.ds(p * C + jt * 128, 128)] = v.astype(BF16)
            return 0

        lax.fori_loop(0, wrows // G, body, 0)

    for i in range(EARLY):
        unpack_w(i)

    def compose(n, u):
        j = n_seq - 1 - n
        map_copy(j, me).wait_recv()
        p = maps[j, 0]
        vr, vi = cmul(p * tr, p * ti, u[0], u[1])
        return vr + maps[j, 1], vi + maps[j, 2]

    ur, ui = lax.fori_loop(0, n_seq - 1 - me, compose, (zero, zero))

    last = me == n_seq - 1

    @pl.when(jnp.logical_not(last))
    def _():
        for c in halo_copies(0):
            c.wait_recv()
        hc = halo_c[...].astype(F32)
        hd = halo_d[...].astype(F32)
        ftmp[0, pl.ds(0, 64), :] = hc
        ftmp[1, pl.ds(0, 64), :] = hd
        vr, vi = ur, ui
        for t in range(3):
            r = ftmp[1, pl.ds(t, NJ, stride=8), :]
            e = jnp.exp(r)
            vr, vi = cmul(e * cr, -e * ci, vr, vi)
            s = scale_of(r)
            g_f[T + t, 0] = s * vr
            g_f[T + t, 1] = s * vi
            a, b = ftmp[0, pl.ds(2 * NJ * t, NJ, stride=2), :], ftmp[0, pl.ds(2 * NJ * t + 1, NJ, stride=2), :]
            vr, vi = vr - a, vi - b

    @pl.when(last)
    def _():
        for t in range(3):
            g_f[T + t, 0] = zero
            g_f[T + t, 1] = zero

    init = [None] * CHUNKS
    for c in reversed(range(CHUNKS)):
        init[c] = (ur, ui)
        ar, ai, sr, si = chunk_maps[c]
        ur, ui = cmul(ar, ai, ur, ui)
        ur, ui = ur + sr, ui + si

    def pass2(n, st):
        j = L - 1 - n
        out = []
        for c in range(CHUNKS):
            ur, ui = st[2 * c : 2 * c + 2]
            t = c * L + j
            a, b = pair(cot_f, t)
            a, b = a + ur, b + ui
            s = g_f[t, 0]
            g_f[t, 0] = s * a
            g_f[t, 1] = s * b
            e = e_f[t]
            out += list(cmul(e * cr, e * ci, a, b))
        return tuple(out)

    lax.fori_loop(0, L, pass2, tuple(v for u in init for v in u))

    cw = [[cw_ref[pl.ds(2 * NJ * k + p, NJ, stride=2), :] for p in range(2)] for k in range(4)]

    def conv(i, _):
        for p in range(2):
            g = [g_f[i * 16 + k, p] for k in range(3)]
            for u in range(16):
                g.append(g_f[i * 16 + u + 3, p])
                f = cw[0][p] * g[u] + cw[1][p] * g[u + 1] + cw[2][p] * g[u + 2] + cw[3][p] * g[u + 3]
                ftmp[p, pl.ds((u // 8) * 8 * NJ + u % 8, NJ, stride=8), :] = f
            for jt in range(NJ):
                v = jnp.concatenate([ftmp[p, pl.ds(jt * 8, 8), :], ftmp[p, pl.ds(8 * NJ + jt * 8, 8), :]], 0)
                feat[pl.ds(pl.multiple_of(i * 16, 16), 16), pl.ds(p * C + jt * 128, 128)] = v.astype(BF16)
        return 0

    lax.fori_loop(0, T // 16, conv, 0)

    own = C // n_seq
    per = 128 // own

    def a2a_copy(src_dev, dst_dev):
        return pltpu.make_async_remote_copy(
            src_ref=featT.at[:, pl.ds(pl.multiple_of(dst_dev * own, own), own), :],
            dst_ref=cm_h.at[:, :, pl.ds(pl.multiple_of(src_dev * T, T), T)],
            send_sem=a2a_s.at[dst_dev], recv_sem=a2a_r.at[src_dev],
            device_id=(dst_dev, ch), device_id_type=MESH)

    local = pltpu.make_async_copy(
        featT.at[:, pl.ds(pl.multiple_of(me * own, own), own), :],
        cm_h.at[:, :, pl.ds(pl.multiple_of(me * T, T), T)], loc_s)

    def turn(s, _):
        jt = lax.rem(me // per + s, NJ)
        for p in range(2):
            blk = feat[:, pl.ds(pl.multiple_of(p * C + jt * 128, 128), 128)]
            featT[p, pl.ds(pl.multiple_of(jt * 128, 128), 128), :] = blk.T

        def send(q, _):
            j = jt * per + lax.rem(me + q, per)

            @pl.when(j != me)
            def _():
                a2a_copy(me, j).start()

            @pl.when(j == me)
            def _():
                local.start()

            return 0

        lax.fori_loop(0, per, send, 0)
        return 0

    lax.fori_loop(0, NJ, turn, 0)

    def taps(i, acc):
        acc = list(acc)
        for p in range(2):
            g = [g_f[i * 4 + k, p] for k in range(3)]
            for u in range(4):
                g.append(g_f[i * 4 + u + 3, p])
                x = x_f[pl.ds(2 * NJ * (i * 4 + u) + p, NJ, stride=2), :]
                for k in range(4):
                    acc[2 * k + p] = acc[2 * k + p] + g[u + k] * x
        return tuple(acc)

    acc = lax.fori_loop(0, T // 4, taps, (zero,) * 8)
    for k in range(4):
        for p in range(2):
            for jt in range(NJ):
                tbuf[2 * NJ * k + 2 * jt + p] = acc[2 * k + p][jt : jt + 1, :]
    trcv[me] = tbuf[me]

    def t1(src_dev, dst_dev):
        return pltpu.make_async_remote_copy(
            src_ref=tbuf.at[dst_dev], dst_ref=trcv.at[src_dev], send_sem=t1_s.at[dst_dev], recv_sem=t1_r.at[src_dev],
            device_id=(dst_dev, ch), device_id_type=MESH)

    def t2(src_dev, dst_dev):
        return pltpu.make_async_remote_copy(
            src_ref=trow, dst_ref=tap_ref.at[src_dev], send_sem=t2_s.at[dst_dev], recv_sem=t2_r.at[src_dev],
            device_id=(dst_dev, ch), device_id_type=MESH)

    def others(fn):
        def body(s, _):
            fn(peer(s))
            return 0

        lax.fori_loop(1, n_seq, body, 0)

    others(lambda j: t1(me, j).start())

    for i in range(EARLY, WCH):
        unpack_w(i)

    nt = D // NT
    half = T // 2

    def par_copy(n):
        cols = pl.ds(pl.multiple_of(n * nt, nt), nt)
        return pltpu.make_async_remote_copy(
            src_ref=part.at[pl.ds(pl.multiple_of(other * half, half), half), cols], dst_ref=part_r.at[:, cols],
            send_sem=par_s.at[n], recv_sem=par_r.at[n], device_id=(me, other), device_id_type=MESH)

    def tile(n, _):
        rows = pl.ds(pl.multiple_of(n * nt, nt), nt)
        y = lax.dot_general(feat[...], wk[rows, :], (((1,), (1,)), ((), ())), preferred_element_type=F32)
        part[:, rows] = y.astype(BF16)
        par_copy(n).start()
        return 0

    lax.fori_loop(0, NT, tile, 0)

    others(lambda j: t1(j, me).wait_recv())
    row = jnp.sum(trcv[...], axis=0)
    trow[...] = row
    tap_ref[me] = row
    others(lambda j: t2(me, j).start())

    def out_copy(n):
        cols = pl.ds(pl.multiple_of(n * nt, nt), nt)
        return pltpu.make_async_copy(obuf.at[:, cols], out_h.at[:, cols], o_sem.at[n])

    def join(n, _):
        par_copy(n).wait_recv()
        cols = pl.ds(pl.multiple_of(n * nt, nt), nt)
        mine = part[pl.ds(pl.multiple_of(ch * half, half), half), cols]
        obuf[:, cols] = (mine.astype(F32) + part_r[:, cols].astype(F32)).astype(BF16)
        out_copy(n).start()
        return 0

    lax.fori_loop(0, NT, join, 0)

    def sent(s, _):
        map_copy(me, me - 1 - s).wait_send()
        return 0

    lax.fori_loop(0, me, sent, 0)

    @pl.when(me > 0)
    def _():
        for c in halo_copies(me - 1):
            c.wait_send()

    def ends(n, _):
        par_copy(n).wait_send()
        out_copy(n).wait()
        return 0

    lax.fori_loop(0, NT, ends, 0)

    def drain(j):
        t1(me, j).wait_send()
        t2(me, j).wait_send()
        a2a_copy(me, j).wait_send()
        t2(j, me).wait_recv()
        a2a_copy(j, me).wait_recv()

    others(drain)
    local.wait()


def solution(mesh):
    n_seq = mesh.shape["seq"]

    def flat(a):
        lead = a.shape[0]
        return a.reshape(lead, 2, -1, 128).transpose(0, 2, 1, 3).reshape(-1, 128)

    def on_device(cotangent, conv_input, decay_rate, angle, conv_weight, in_weight):
        T, _, C = cotangent.shape
        D = in_weight.shape[0]
        NJ = C // 128
        dec = decay_rate.reshape(T // 8, 8, NJ, 128).transpose(0, 2, 1, 3).reshape(-1, 128)
        dma = pltpu.SemaphoreType.DMA
        ANY = pl.BlockSpec(memory_space=pl.ANY)
        V = pl.BlockSpec(memory_space=pltpu.VMEM)
        rows = 8 * NJ
        out, cm, tap = pl.pallas_call(
            functools.partial(kernel, n_seq, T, C, D),
            out_shape=(
                jax.ShapeDtypeStruct((T // 2, D), BF16),
                jax.ShapeDtypeStruct((2, C // n_seq, T * n_seq), BF16),
                jax.ShapeDtypeStruct((rows, 1, 128), F32),
            ),
            in_specs=[ANY, ANY, ANY, V, V, ANY],
            out_specs=(ANY, ANY, V),
            scratch_shapes=[
                pltpu.VMEM((T * 2 * NJ, 128), BF16),
                pltpu.VMEM((T * 2 * NJ, 128), BF16),
                pltpu.VMEM((T * NJ, 128), BF16),
                pltpu.VMEM((D * 2 * NJ, 128), BF16),
                pltpu.VMEM((64, 128), BF16),
                pltpu.VMEM((64, 128), BF16),
                pltpu.VMEM((T * 2 * NJ, 128), F32),
                pltpu.VMEM((T * 2 * NJ, 128), F32),
                pltpu.VMEM((T * NJ, 128), F32),
                pltpu.VMEM((T, NJ, 128), F32),
                pltpu.VMEM((T + 3, 2, NJ, 128), F32),
                pltpu.VMEM((2, 32 * NJ, 128), F32),
                pltpu.VMEM((D, 2 * C), BF16),
                pltpu.VMEM((2, 16 * NJ, 128), F32),
                pltpu.VMEM((T, 2 * C), BF16),
                pltpu.VMEM((2, C, T), BF16),
                pltpu.VMEM((3, NJ, 128), F32),
                pltpu.VMEM((n_seq, 3, NJ, 128), F32),
                pltpu.VMEM((T, D), BF16),
                pltpu.VMEM((T // 2, D), BF16),
                pltpu.VMEM((T // 2, D), BF16),
                pltpu.VMEM((rows, 1, 128), F32),
                pltpu.VMEM((n_seq, 1, 128), F32),
                pltpu.VMEM((1, 128), F32),
                dma((3,)), dma((WCH,)), dma((2,)), dma((2,)),
                dma((n_seq,)), dma((n_seq,)), dma((n_seq,)), dma((n_seq,)), dma,
                dma((NT,)), dma((NT,)),
                dma((n_seq,)), dma((n_seq,)), dma((n_seq,)), dma((n_seq,)), dma((NT,)),
            ],
            compiler_params=pltpu.CompilerParams(
                collective_id=0, has_side_effects=True, vmem_limit_bytes=62 * 1024 * 1024),
        )(flat(cotangent), flat(conv_input), dec, angle.reshape(NJ, 128), flat(conv_weight), flat(in_weight))
        tap = tap.reshape(4, NJ, 2, 128).transpose(0, 2, 1, 3).reshape(4, 2, C)
        return out, cm, tap

    in_specs = (
        P("seq", None, "ch"),
        P("seq", None, "ch"),
        P("seq", "ch"),
        P("ch"),
        P(None, None, "ch"),
        P(None, None, "ch"),
    )
    out_specs = (P(("seq", "ch"), None), P(None, ("ch", "seq"), None), P(None, None, "ch"))
    return jax.shard_map(on_device, mesh=mesh, in_specs=in_specs, out_specs=out_specs, check_vma=False)
```

time: 1340 us -> 74.6 us (0.06)
  blocking collectives: 1040 us -> 0 us
  local copies, waits for them, and re-layouts: 205 us -> 5.92 us
  Pallas kernels: 0 us -> 67.8 us
  other arithmetic: 44.8 us -> 0 us
  between operations: 15.7 us -> 0.64 us
    all_gather x4 -> x0, blocking collectives: 690 us -> none  [prefix(): pieces = jax.tree.map(lambda part: lax.all_gather(part, axis), value)]
    psum x1 -> x0, blocking collectives: 349 us -> none  [on_device(): tap_grad = lax.psum(jnp.stack(taps, 0), 'seq')]
    dynamic_slice x126 -> x0, local copies, waits for them, and re-layouts: 99.6 us -> none  [hop(): longer = join(total, jax.tree.map(lambda part: part[position], pieces))]
    pallas_call x0 -> x1, Pallas kernels: none -> 67.8 us  [on_device(): pl.pallas_call(functools.partial(kernel, n_seq, T, C, D), out_shape=(jax....]
    slice x114 -> x0, local copies, waits for them, and re-layouts: 38.1 us -> none  [the longest x110 36.3 us: local_block(): scanned = lax.associative_scan(compose, elements, axis=0)]
    rev x10 -> x0, local copies, waits for them, and re-layouts: 31.1 us -> none  [the longest x4 19.9 us: local_block(): member[::-1]]
    pad x56 -> x0, local copies, waits for them, and re-layouts: 24.1 us -> none  [local_block(): scanned = lax.associative_scan(compose, elements, axis=0)]
    add x51 -> x0, other arithmetic: 23.4 us -> none  [the longest x30 16.4 us: local_block(): scanned = lax.associative_scan(compose, elements, axis=0)]
  transfers between devices with their start and end apart: 4 -> 0, of which waited for: 1 -> 0; matrix products, arithmetic and copies ran while one was open for 18% -> 0% of each run, Pallas kernels for 0% -> 0%
where the time goes in v1:
time: 74.6 us; the launch traced here: 74.3 us
  Pallas kernels  67.8 us (91%)
  local copies, waits for them, and re-layouts  5.92 us (8%)
    pallas_call x1, Pallas kernels, on_device(): pl.pallas_call(functools.partial(kernel, n_seq, T, C, D), out_shape=(jax....  67.8 us
    unnamed x3, local copies, waits for them, and re-layouts  5.92 us

profile of v1, /device:TPU:0, one launch (start us, length us, event | category | flops | bytes accessed | tf_op | source)
XLA Modules:
  0.0 74.3 jit_solution(17352280926761576059)
XLA Ops:
  0.6 67.8 %shard_map.85 = (bf16[128,4096]{1,0:T(8,128)(2,1)}, bf16[2,16,16384]{2,1,0:T(8,128)(2,1)}, f32[64,1,128]{2,1,0:T(1,128)}) custom-call(bf16[4096,128]{1,0:T(8,128)(2,1)} %bitcast.32, bf16[4096,128]{1,0:T(8,128)(2,1)} %bitcast.33, bf16[2048,128]{1,0:T(8,128)(2,1)} %bitcast.34, f32[8,128]{1,0:T(8,128)} %bitcast.37, f32[64,128]{1,0:T(8,128)} %bitcast.35, ...), custom_call_target="tpu_custom_call" | custom-call | tf_op jit(solution)/shard_map/pallas_call | solution.py:433
  68.4 2.3 %copy.17 = bf16[128,4096]{1,0:T(8,128)(2,1)} copy(bf16[128,4096]{1,0:T(8,128)(2,1)} %get-tuple-element.12) | data formatting | bytes 2097152
  70.7 2.3 %copy.18 = bf16[2,16,16384]{2,1,0:T(8,128)(2,1)} copy(bf16[2,16,16384]{2,1,0:T(8,128)(2,1)} %get-tuple-element.13) | data formatting | bytes 2097152
  72.9 1.4 %copy.19 = f32[4,2,1024]{2,1,0:T(2,128)} copy(f32[4,2,1024]{2,1,0:T(2,128)} %bitcast.36) | data formatting | bytes 65536

commit v2 on v1

v2 whole, which is shorter than its diff:
```python
import functools

import jax
import jax.numpy as jnp
from jax import lax
from jax.experimental import pallas as pl
from jax.experimental.pallas import tpu as pltpu
from jax.sharding import PartitionSpec as P

MESH = pl.DeviceIdType.MESH
F32 = jnp.float32
BF16 = jnp.bfloat16
CHUNKS = 8
WCH = 8
W1, W2, W3 = 1, 4, 7
UNR = 2
NT = 8
RING = 4
STAGES = 3


def cmul(ar, ai, br, bi):
    return ar * br - ai * bi, ar * bi + ai * br


def scale_of(r):
    y = 0.25 * r
    q = y * (1.0 - y * (1 / 2) * (1.0 - y * (1 / 3) * (1.0 - y * (1 / 4) * (1.0 - y * (1 / 5) * (1.0 - y * (1 / 6))))))
    q = q * (2.0 - q)
    q = q * (2.0 - q)
    q = q * (2.0 - q)
    return jnp.sqrt(q)


def kernel(
    n_seq, T, C, D,
    cot_h, x_h, dec_h, ang_ref, cw_ref, w_h,
    out_h, cm_h, tap_ref,
    cot_b, x_b, dec_b, w_b, halo_c, halo_d,
    cot_f, x_f, e_f, sc_f, g_f, wtmp, wk, ftmp, feat, featT,
    mapv, maps, part, part_r, obuf, tbuf, trcv, trow,
    in_sem, w_sem, halo_s, halo_r, map_s, map_r, a2a_s, a2a_r, loc_s, par_s, par_r, t1_s, t1_r, t2_s, t2_r, o_sem,
):
    me = lax.axis_index("seq")
    ch = lax.axis_index("ch")
    other = 1 - ch
    NJ = C // 128
    L = T // CHUNKS
    strides = [RING**k for k in range(STAGES)]
    place = [lax.rem(me // st, RING) for st in strides]

    def ring(k, s):
        return me + (lax.rem(place[k] + s, RING) - place[k]) * strides[k]

    barrier = pltpu.get_barrier_semaphore()

    def greet(dev, core):
        pl.semaphore_signal(barrier, inc=1, device_id=(dev, core), device_id_type=MESH)

    for k in range(STAGES):
        for s in range(1, RING):
            greet(ring(k, s), ch)
    before, after = lax.rem(me + n_seq - 1, n_seq), lax.rem(me + 1, n_seq)
    greet(before, ch)
    greet(after, ch)
    greet(me, other)
    greetings = STAGES * (RING - 1) + 3

    c_dec = pltpu.make_async_copy(dec_h, dec_b, in_sem.at[0])
    c_cot = pltpu.make_async_copy(cot_h, cot_b, in_sem.at[1])
    c_x = pltpu.make_async_copy(x_h, x_b, in_sem.at[2])
    c_dec.start()
    c_cot.start()
    c_x.start()
    wrows = w_h.shape[0] // WCH

    def w_copy(i):
        return pltpu.make_async_copy(
            w_h.at[pl.ds(i * wrows, wrows)], w_b.at[pl.ds(i * wrows, wrows)], w_sem.at[i])

    for i in range(WCH):
        w_copy(i).start()

    ang = ang_ref[...]
    cr = jnp.cos(ang)
    ci = -jnp.sin(ang)

    def rowwise(src, dst, fn):
        def body(i, _):
            r = pl.multiple_of(i * 64, 64)
            dst[pl.ds(r, 64), :] = fn(src[pl.ds(r, 64), :].astype(F32))
            return 0

        lax.fori_loop(0, src.shape[0] // 64, body, 0)

    def pair(ref, t):
        return ref[pl.ds(2 * NJ * t, NJ, stride=2), :], ref[pl.ds(2 * NJ * t + 1, NJ, stride=2), :]

    c_dec.wait()
    rowwise(dec_b, e_f, lambda r: jnp.exp(-r))
    c_cot.wait()
    rowwise(cot_b, cot_f, lambda v: v)

    zero = jnp.zeros((NJ, 128), F32)
    one = jnp.ones((NJ, 128), F32)

    def at(t8, u):
        return pl.ds(8 * NJ * t8 + u, NJ, stride=8)

    def pass1(n, st):
        st = list(st)
        for u in reversed(range(8)):
            for c in range(CHUNKS):
                t8 = c * (L // 8) + L // 8 - 1 - n
                ur, ui, p = st[3 * c : 3 * c + 3]
                e = e_f[at(t8, u), :]
                a, b = pair(cot_f, t8 * 8 + u)
                ur, ui = cmul(e * cr, e * ci, a + ur, b + ui)
                st[3 * c : 3 * c + 3] = ur, ui, p * e
        return tuple(st)

    st = lax.fori_loop(0, L // 8, pass1, (zero, zero, one) * CHUNKS)

    def power(ar, ai, n):
        while n > 1:
            ar, ai = ar * ar - ai * ai, 2.0 * ar * ai
            n //= 2
        return ar, ai

    lr, li = power(cr, ci, L)
    rot = power(lr, li, CHUNKS)
    chunk_maps = []
    for c in range(CHUNKS):
        ur, ui, p = st[3 * c : 3 * c + 3]
        chunk_maps.append((p * lr, p * li, ur, ui))
    br, bi = zero, zero
    total = one
    for c in reversed(range(CHUNKS)):
        ar, ai, sr, si = chunk_maps[c]
        br, bi = cmul(ar, ai, br, bi)
        br, bi = br + sr, bi + si
        total = total * st[3 * c + 2]

    pl.semaphore_wait(barrier, greetings)

    def halo_copies(dst_dev):
        return [
            pltpu.make_async_remote_copy(
                src_ref=s, dst_ref=d, send_sem=halo_s.at[i], recv_sem=halo_r.at[i],
                device_id=(dst_dev, ch), device_id_type=MESH)
            for i, (s, d) in enumerate(
                ((cot_b.at[pl.ds(0, 64)], halo_c), (dec_b.at[pl.ds(0, 64)], halo_d)))
        ]

    def map_copy(k, s):
        return pltpu.make_async_remote_copy(
            src_ref=mapv.at[k], dst_ref=maps.at[k, place[k]], send_sem=map_s.at[k, s], recv_sem=map_r.at[k, RING - s],
            device_id=(ring(k, s), ch), device_id_type=MESH)

    def send_map(k, p, br, bi):
        for i, v in enumerate((p, br, bi)):
            mapv[k, i] = v
            maps[k, place[k], i] = v
        for s in range(1, RING):
            map_copy(k, s).start()

    def stage(k, rot):
        for s in range(1, RING):
            map_copy(k, s).wait_recv()
        ar, ai, br, bi, p = one, zero, zero, zero, one
        mine = None
        for j in reversed(range(RING)):
            here = place[k] == j
            now = (ar, ai, br, bi)
            mine = now if mine is None else tuple(jnp.where(here, x, y) for x, y in zip(now, mine))
            q = maps[k, j, 0]
            vr, vi = q * rot[0], q * rot[1]
            br, bi = cmul(vr, vi, br, bi)
            br, bi = br + maps[k, j, 1], bi + maps[k, j, 2]
            if j > 0:
                ar, ai = cmul(vr, vi, ar, ai)
            p = p * q
        return mine, (p, br, bi)

    send_map(0, total, br, bi)

    @pl.when(me > 0)
    def _():
        for c in halo_copies(before):
            c.start()

    G = 16 * 2 * NJ

    def unpack_w(i):
        w_copy(i).wait()
        base = i * (wrows // (2 * NJ))

        def body(k, _):
            for v in range(UNR):
                d0 = pl.multiple_of(base + k * (16 * UNR) + v * 16, 16)
                tmp = wtmp.at[v]
                tmp[...] = w_b[pl.ds(pl.multiple_of(d0 * 2 * NJ, G), G), :].astype(F32)
                for p in range(2):
                    for jt in range(NJ):
                        x = tmp[pl.ds(2 * jt + p, 16, stride=2 * NJ), :]
                        wk[p * NJ + jt, pl.ds(d0, 16), :] = x.astype(BF16)
            return 0

        lax.fori_loop(0, wrows // (G * UNR), body, 0)

    rowwise(dec_b, sc_f, scale_of)
    c_x.wait()
    rowwise(x_b, x_f, lambda v: v)
    for i in range(0, W1):
        unpack_w(i)

    later0, whole0 = stage(0, rot)
    send_map(1, *whole0)
    for i in range(W1, W2):
        unpack_w(i)
    rot1 = power(*rot, RING)
    later1, whole1 = stage(1, rot1)
    send_map(2, *whole1)
    for i in range(W2, W3):
        unpack_w(i)
    later2, _ = stage(2, power(*rot1, RING))

    ur, ui = later2[2], later2[3]
    for ar, ai, br, bi in (later1, later0):
        ur, ui = cmul(ar, ai, ur, ui)
        ur, ui = ur + br, ui + bi

    last = me == n_seq - 1

    @pl.when(jnp.logical_not(last))
    def _():
        for c in halo_copies(before):
            c.wait_recv()
        ftmp[0, pl.ds(0, 64), :] = halo_c[...].astype(F32)
        ftmp[1, pl.ds(0, 64), :] = halo_d[...].astype(F32)
        vr, vi = ur, ui
        for t in range(3):
            r = ftmp[1, pl.ds(t, NJ, stride=8), :]
            e = jnp.exp(r)
            vr, vi = cmul(e * cr, -e * ci, vr, vi)
            s = scale_of(r)
            g_f[T + t, 0] = s * vr
            g_f[T + t, 1] = s * vi
            a, b = pair(ftmp.at[0], t)
            vr, vi = vr - a, vi - b

    @pl.when(last)
    def _():
        for t in range(3):
            g_f[T + t, 0] = zero
            g_f[T + t, 1] = zero

    init = [None] * CHUNKS
    for c in reversed(range(CHUNKS)):
        init[c] = (ur, ui)
        ar, ai, sr, si = chunk_maps[c]
        ur, ui = cmul(ar, ai, ur, ui)
        ur, ui = ur + sr, ui + si

    def pass2(n, st):
        st = list(st)
        for u in reversed(range(8)):
            for c in range(CHUNKS):
                t8 = c * (L // 8) + L // 8 - 1 - n
                t = t8 * 8 + u
                ur, ui = st[2 * c : 2 * c + 2]
                a, b = pair(cot_f, t)
                a, b = a + ur, b + ui
                s = sc_f[at(t8, u), :]
                g_f[t, 0] = s * a
                g_f[t, 1] = s * b
                e = e_f[at(t8, u), :]
                st[2 * c : 2 * c + 2] = cmul(e * cr, e * ci, a, b)
        return tuple(st)

    lax.fori_loop(0, L // 8, pass2, tuple(v for u in init for v in u))

    def taps(i, acc):
        acc = list(acc)
        for p in range(2):
            g = [g_f[i * 8 + k, p] for k in range(3)]
            for u in range(8):
                g.append(g_f[i * 8 + u + 3, p])
                x = x_f[pl.ds(2 * NJ * (i * 8 + u) + p, NJ, stride=2), :]
                for k in range(4):
                    acc[2 * k + p] = acc[2 * k + p] + g[u + k] * x
        return tuple(acc)

    acc = lax.fori_loop(0, T // 8, taps, (zero,) * 8)
    for k in range(4):
        for p in range(2):
            for jt in range(NJ):
                tbuf[2 * NJ * k + 2 * jt + p] = acc[2 * k + p][jt : jt + 1, :]
    trcv[me] = tbuf[me]

    def t1(dst_dev):
        return pltpu.make_async_remote_copy(
            src_ref=tbuf.at[dst_dev], dst_ref=trcv.at[me], send_sem=t1_s, recv_sem=t1_r,
            device_id=(dst_dev, ch), device_id_type=MESH)

    def t2(dst_dev):
        return pltpu.make_async_remote_copy(
            src_ref=trow, dst_ref=tap_ref.at[me], send_sem=t2_s, recv_sem=t2_r,
            device_id=(dst_dev, ch), device_id_type=MESH)

    def others(fn):
        def body(s, _):
            j = me + s
            fn(jnp.where(j >= n_seq, j - n_seq, j))
            return 0

        lax.fori_loop(1, n_seq, body, 0)

    others(lambda j: t1(j).start())

    cw = [[cw_ref[pl.ds(2 * NJ * k + p, NJ, stride=2), :] for p in range(2)] for k in range(4)]

    def conv(i, _):
        for p in range(2):
            g = [g_f[i * 16 + k, p] for k in range(3)]
            for u in range(16):
                g.append(g_f[i * 16 + u + 3, p])
                f = cw[0][p] * g[u] + cw[1][p] * g[u + 1] + cw[2][p] * g[u + 2] + cw[3][p] * g[u + 3]
                ftmp[p, pl.ds((u // 8) * 8 * NJ + u % 8, NJ, stride=8), :] = f
            for jt in range(NJ):
                v = jnp.concatenate([ftmp[p, pl.ds(jt * 8, 8), :], ftmp[p, pl.ds(8 * NJ + jt * 8, 8), :]], 0)
                feat[p * NJ + jt, pl.ds(pl.multiple_of(i * 16, 16), 16), :] = v.astype(BF16)
        return 0

    lax.fori_loop(0, T // 16, conv, 0)

    own = C // n_seq
    per = 128 // own

    def a2a_src(dst_dev):
        return featT.at[:, pl.ds(pl.multiple_of(dst_dev * own, own), own), :]

    cm_mine = cm_h.at[:, :, pl.ds(pl.multiple_of(me * T, T), T)]

    def a2a_copy(dst_dev):
        return pltpu.make_async_remote_copy(
            src_ref=a2a_src(dst_dev), dst_ref=cm_mine, send_sem=a2a_s, recv_sem=a2a_r,
            device_id=(dst_dev, ch), device_id_type=MESH)

    local = pltpu.make_async_copy(a2a_src(me), cm_mine, loc_s)

    def turn(s, _):
        jt = me // per + s
        jt = jnp.where(jt >= NJ, jt - NJ, jt)
        for p in range(2):
            featT[p, pl.ds(pl.multiple_of(jt * 128, 128), 128), :] = feat[p * NJ + jt].T
        for q in range(per):
            j = jt * per + q

            @pl.when(j != me)
            def _():
                a2a_copy(j).start()

        return 0

    lax.fori_loop(0, NJ, turn, 0)
    local.start()

    for i in range(W3, WCH):
        unpack_w(i)

    nt = D // NT
    half = T // 2

    def par_copy(n):
        cols = pl.ds(pl.multiple_of(n * nt, nt), nt)
        return pltpu.make_async_remote_copy(
            src_ref=part.at[pl.ds(pl.multiple_of(other * half, half), half), cols], dst_ref=part_r.at[:, cols],
            send_sem=par_s.at[n], recv_sem=par_r.at[n], device_id=(me, other), device_id_type=MESH)

    def tile(n, _):
        rows = pl.ds(pl.multiple_of(n * nt, nt), nt)
        lhs = jnp.concatenate([feat[i] for i in range(2 * NJ)], 1)
        rhs = jnp.concatenate([wk[i, rows, :] for i in range(2 * NJ)], 1)
        y = lax.dot_general(lhs, rhs, (((1,), (1,)), ((), ())), preferred_element_type=F32)
        part[:, rows] = y.astype(BF16)
        par_copy(n).start()
        return 0

    lax.fori_loop(0, NT // 2, tile, 0)

    def all_but_one(ref, sem):
        part_of = ref.at[pl.ds(0, n_seq - 1)]
        return pltpu.make_async_copy(part_of, part_of, sem)

    all_but_one(trcv, t1_r).wait()
    row = jnp.sum(trcv[...], axis=0)
    trow[...] = row
    tap_ref[me] = row
    others(lambda j: t2(j).start())

    lax.fori_loop(NT // 2, NT, tile, 0)

    def out_copy(n):
        cols = pl.ds(pl.multiple_of(n * nt, nt), nt)
        return pltpu.make_async_copy(obuf.at[:, cols], out_h.at[:, cols], o_sem.at[n])

    def join(n, _):
        par_copy(n).wait_recv()
        cols = pl.ds(pl.multiple_of(n * nt, nt), nt)
        mine = part[pl.ds(pl.multiple_of(ch * half, half), half), cols]
        obuf[:, cols] = (mine.astype(F32) + part_r[:, cols].astype(F32)).astype(BF16)
        out_copy(n).start()
        return 0

    lax.fori_loop(0, NT, join, 0)

    for k in range(STAGES):
        for s in range(1, RING):
            map_copy(k, s).wait_send()

    @pl.when(me > 0)
    def _():
        for c in halo_copies(before):
            c.wait_send()

    def ends(n, _):
        par_copy(n).wait_send()
        out_copy(n).wait()
        return 0

    lax.fori_loop(0, NT, ends, 0)
    all_but_one(trcv, t1_s).wait()
    all_but_one(trcv, t2_s).wait()
    all_but_one(tap_ref, t2_r).wait()
    local.wait()
    sent = featT.at[:, pl.ds(0, C - own), :]
    pltpu.make_async_copy(sent, sent, a2a_s).wait()
    came = cm_h.at[:, :, pl.ds(0, T * (n_seq - 1))]
    pltpu.make_async_copy(came, came, a2a_r).wait()


def solution(mesh):
    n_seq = mesh.shape["seq"]

    def flat(a):
        lead = a.shape[0]
        return a.reshape(lead, 2, -1, 128).transpose(0, 2, 1, 3).reshape(-1, 128)

    def on_device(cotangent, conv_input, decay_rate, angle, conv_weight, in_weight):
        T, _, C = cotangent.shape
        D = in_weight.shape[0]
        NJ = C // 128
        dec = decay_rate.reshape(T // 8, 8, NJ, 128).transpose(0, 2, 1, 3).reshape(-1, 128)
        dma = pltpu.SemaphoreType.DMA
        ANY = pl.BlockSpec(memory_space=pl.ANY)
        V = pl.BlockSpec(memory_space=pltpu.VMEM)
        rows = 8 * NJ
        out, cm, tap = pl.pallas_call(
            functools.partial(kernel, n_seq, T, C, D),
            out_shape=(
                jax.ShapeDtypeStruct((T // 2, D), BF16),
                jax.ShapeDtypeStruct((2, C // n_seq, T * n_seq), BF16),
                jax.ShapeDtypeStruct((rows, 1, 128), F32),
            ),
            in_specs=[ANY, ANY, ANY, V, V, ANY],
            out_specs=(ANY, ANY, V),
            scratch_shapes=[
                pltpu.VMEM((T * 2 * NJ, 128), BF16),
                pltpu.VMEM((T * 2 * NJ, 128), BF16),
                pltpu.VMEM((T * NJ, 128), BF16),
                pltpu.VMEM((D * 2 * NJ, 128), BF16),
                pltpu.VMEM((64, 128), BF16),
                pltpu.VMEM((64, 128), BF16),
                pltpu.VMEM((T * 2 * NJ, 128), F32),
                pltpu.VMEM((T * 2 * NJ, 128), F32),
                pltpu.VMEM((T * NJ, 128), F32),
                pltpu.VMEM((T * NJ, 128), F32),
                pltpu.VMEM((T + 3, 2, NJ, 128), F32),
                pltpu.VMEM((UNR, 32 * NJ, 128), F32),
                pltpu.VMEM((2 * NJ, D, 128), BF16),
                pltpu.VMEM((2, 16 * NJ, 128), F32),
                pltpu.VMEM((2 * NJ, T, 128), BF16),
                pltpu.VMEM((2, C, T), BF16),
                pltpu.VMEM((STAGES, 3, NJ, 128), F32),
                pltpu.VMEM((STAGES, RING, 3, NJ, 128), F32),
                pltpu.VMEM((T, D), BF16),
                pltpu.VMEM((T // 2, D), BF16),
                pltpu.VMEM((T // 2, D), BF16),
                pltpu.VMEM((rows, 1, 128), F32),
                pltpu.VMEM((n_seq, 1, 128), F32),
                pltpu.VMEM((1, 128), F32),
                dma((3,)), dma((WCH,)), dma((2,)), dma((2,)),
                dma((STAGES, RING)), dma((STAGES, RING)), dma, dma, dma,
                dma((NT,)), dma((NT,)),
                dma, dma, dma, dma, dma((NT,)),
            ],
            compiler_params=pltpu.CompilerParams(
                collective_id=0, has_side_effects=True, vmem_limit_bytes=62 * 1024 * 1024),
        )(flat(cotangent), flat(conv_input), dec, angle.reshape(NJ, 128), flat(conv_weight), flat(in_weight))
        tap = tap.reshape(4, NJ, 2, 128).transpose(0, 2, 1, 3).reshape(4, 2, C)
        return out, cm, tap

    in_specs = (
        P("seq", None, "ch"),
        P("seq", None, "ch"),
        P("seq", "ch"),
        P("ch"),
        P(None, None, "ch"),
        P(None, None, "ch"),
    )
    out_specs = (P(("seq", "ch"), None), P(None, ("ch", "seq"), None), P(None, None, "ch"))
    return jax.shard_map(on_device, mesh=mesh, in_specs=in_specs, out_specs=out_specs, check_vma=False)
```

time: 74.6 us -> 52.7 us (0.71)
  Pallas kernels: 67.8 us -> 45.7 us
    pallas_call x1, Pallas kernels: 67.8 us -> 45.7 us  [on_device(): pl.pallas_call(functools.partial(kernel, n_seq, T, C, D), out_shape=(jax....]
where the time goes in v2:
time: 52.7 us; the launch traced here: 52.3 us
  Pallas kernels  45.7 us (87%)
  local copies, waits for them, and re-layouts  5.92 us (11%)
  between operations  0.64 us (1%)
    pallas_call x1, Pallas kernels, on_device(): pl.pallas_call(functools.partial(kernel, n_seq, T, C, D), out_shape=(jax....  45.7 us
    unnamed x3, local copies, waits for them, and re-layouts  5.92 us

profile of v2, /device:TPU:0, one launch (start us, length us, event | category | flops | bytes accessed | tf_op | source)
XLA Modules:
  0.0 52.3 jit_solution(8541110245810639236)
XLA Ops:
  0.6 45.7 %shard_map.85 = (bf16[128,4096]{1,0:T(8,128)(2,1)}, bf16[2,16,16384]{2,1,0:T(8,128)(2,1)}, f32[64,1,128]{2,1,0:T(1,128)}) custom-call(bf16[4096,128]{1,0:T(8,128)(2,1)} %bitcast.32, bf16[4096,128]{1,0:T(8,128)(2,1)} %bitcast.33, bf16[2048,128]{1,0:T(8,128)(2,1)} %bitcast.34, f32[8,128]{1,0:T(8,128)} %bitcast.37, f32[64,128]{1,0:T(8,128)} %bitcast.35, ...), custom_call_target="tpu_custom_call" | custom-call | tf_op jit(solution)/shard_map/pallas_call | solution.py:459
  46.4 2.3 %copy.17 = bf16[128,4096]{1,0:T(8,128)(2,1)} copy(bf16[128,4096]{1,0:T(8,128)(2,1)} %get-tuple-element.12) | data formatting | bytes 2097152
  48.7 2.3 %copy.18 = bf16[2,16,16384]{2,1,0:T(8,128)(2,1)} copy(bf16[2,16,16384]{2,1,0:T(8,128)(2,1)} %get-tuple-element.13) | data formatting | bytes 2097152
  50.9 1.4 %copy.19 = f32[4,2,1024]{2,1,0:T(2,128)} copy(f32[4,2,1024]{2,1,0:T(2,128)} %bitcast.36) | data formatting | bytes 65536

commit v3 on v2

--- a/solution.py
+++ b/solution.py
@@ -12,8 +12,10 @@
 BF16 = jnp.bfloat16
 CHUNKS = 8
 WCH = 8
-W1, W2, W3 = 1, 4, 7
+WSLOT = 4
+W1, W2, W3 = 1, 3, 5
 UNR = 2
+FIN = 4
 NT = 8
 RING = 4
 STAGES = 3
@@ -34,11 +36,11 @@
 
 def kernel(
     n_seq, T, C, D,
-    cot_h, x_h, dec_h, ang_ref, cw_ref, w_h,
-    out_h, cm_h, tap_ref,
-    cot_b, x_b, dec_b, w_b, halo_c, halo_d,
+    cot_h, x_h, dec_h, ang_h, cw_h, w_h,
+    mine_h, part_r, cm_h, tap_ref,
+    ang_ref, cw_ref, cot_b, x_b, dec_b, w_b, halo_c, halo_d,
     cot_f, x_f, e_f, sc_f, g_f, wtmp, wk, ftmp, feat, featT,
-    mapv, maps, part, part_r, obuf, tbuf, trcv, trow,
+    mapv, maps, part, tbuf, trcv, trow,
     in_sem, w_sem, halo_s, halo_r, map_s, map_r, a2a_s, a2a_r, loc_s, par_s, par_r, t1_s, t1_r, t2_s, t2_r, o_sem,
 ):
     me = lax.axis_index("seq")
@@ -69,21 +71,22 @@
     c_dec = pltpu.make_async_copy(dec_h, dec_b, in_sem.at[0])
     c_cot = pltpu.make_async_copy(cot_h, cot_b, in_sem.at[1])
     c_x = pltpu.make_async_copy(x_h, x_b, in_sem.at[2])
+    c_ang = pltpu.make_async_copy(ang_h, ang_ref, in_sem.at[3])
+    c_cw = pltpu.make_async_copy(cw_h, cw_ref, in_sem.at[4])
     c_dec.start()
+    c_ang.start()
     c_cot.start()
     c_x.start()
+    c_cw.start()
     wrows = w_h.shape[0] // WCH
 
     def w_copy(i):
         return pltpu.make_async_copy(
-            w_h.at[pl.ds(i * wrows, wrows)], w_b.at[pl.ds(i * wrows, wrows)], w_sem.at[i])
-
-    for i in range(WCH):
+            w_h.at[pl.ds(i * wrows, wrows)], w_b.at[i % WSLOT], w_sem.at[i % WSLOT])
+
+    for i in range(WSLOT):
         w_copy(i).start()
 
-    ang = ang_ref[...]
-    cr = jnp.cos(ang)
-    ci = -jnp.sin(ang)
 
     def rowwise(src, dst, fn):
         def body(i, _):
@@ -98,6 +101,10 @@
 
     c_dec.wait()
     rowwise(dec_b, e_f, lambda r: jnp.exp(-r))
+    c_ang.wait()
+    ang = ang_ref[...]
+    cr = jnp.cos(ang)
+    ci = -jnp.sin(ang)
     c_cot.wait()
     rowwise(cot_b, cot_f, lambda v: v)
 
@@ -189,24 +196,30 @@
         for c in halo_copies(before):
             c.start()
 
-    G = 16 * 2 * NJ
+    G = 2 * NJ
 
     def unpack_w(i):
         w_copy(i).wait()
-        base = i * (wrows // (2 * NJ))
+        base = i * (wrows // G)
+        src = w_b.at[i % WSLOT]
 
         def body(k, _):
             for v in range(UNR):
-                d0 = pl.multiple_of(base + k * (16 * UNR) + v * 16, 16)
-                tmp = wtmp.at[v]
-                tmp[...] = w_b[pl.ds(pl.multiple_of(d0 * 2 * NJ, G), G), :].astype(F32)
+                g = k * UNR + v
+                d0 = pl.multiple_of(base + g * 16, 16)
+                for d in range(16):
+                    x = src[pl.ds(pl.multiple_of((g * 16 + d) * G, G), G), :].astype(F32)
+                    for h in range(2):
+                        wtmp[v, h, pl.ds(d * 8, 8), :] = x[h * 8 : h * 8 + 8, :]
                 for p in range(2):
                     for jt in range(NJ):
-                        x = tmp[pl.ds(2 * jt + p, 16, stride=2 * NJ), :]
+                        x = wtmp[v, jt // 4, pl.ds(2 * (jt % 4) + p, 16, stride=8), :]
                         wk[p * NJ + jt, pl.ds(d0, 16), :] = x.astype(BF16)
             return 0
 
-        lax.fori_loop(0, wrows // (G * UNR), body, 0)
+        lax.fori_loop(0, wrows // (G * 16 * UNR), body, 0)
+        if i + WSLOT < WCH:
+            w_copy(i + WSLOT).start()
 
     rowwise(dec_b, sc_f, scale_of)
     c_x.wait()
@@ -318,6 +331,7 @@
 
     others(lambda j: t1(j).start())
 
+    c_cw.wait()
     cw = [[cw_ref[pl.ds(2 * NJ * k + p, NJ, stride=2), :] for p in range(2)] for k in range(4)]
 
     def conv(i, _):
@@ -401,19 +415,8 @@
 
     lax.fori_loop(NT // 2, NT, tile, 0)
 
-    def out_copy(n):
-        cols = pl.ds(pl.multiple_of(n * nt, nt), nt)
-        return pltpu.make_async_copy(obuf.at[:, cols], out_h.at[:, cols], o_sem.at[n])
-
-    def join(n, _):
-        par_copy(n).wait_recv()
-        cols = pl.ds(pl.multiple_of(n * nt, nt), nt)
-        mine = part[pl.ds(pl.multiple_of(ch * half, half), half), cols]
-        obuf[:, cols] = (mine.astype(F32) + part_r[:, cols].astype(F32)).astype(BF16)
-        out_copy(n).start()
-        return 0
-
-    lax.fori_loop(0, NT, join, 0)
+    mine = pltpu.make_async_copy(part.at[pl.ds(pl.multiple_of(ch * half, half), half), :], mine_h, o_sem)
+    mine.start()
 
     for k in range(STAGES):
         for s in range(1, RING):
@@ -425,11 +428,11 @@
             c.wait_send()
 
     def ends(n, _):
-        par_copy(n).wait_send()
-        out_copy(n).wait()
+        par_copy(n).wait()
         return 0
 
     lax.fori_loop(0, NT, ends, 0)
+    mine.wait()
     all_but_one(trcv, t1_s).wait()
     all_but_one(trcv, t2_s).wait()
     all_but_one(tap_ref, t2_r).wait()
@@ -438,6 +441,21 @@
     pltpu.make_async_copy(sent, sent, a2a_s).wait()
     came = cm_h.at[:, :, pl.ds(0, T * (n_seq - 1))]
     pltpu.make_async_copy(came, came, a2a_r).wait()
+
+
+def finish(mine, part, cm, tap, out_h, cm_h, tap_h, out, sem):
+    rows = mine.shape[0] // FIN
+    copies = [pltpu.make_async_copy(cm.at[p], cm_h.at[p], sem.at[FIN + p]) for p in range(2)]
+    copies.append(pltpu.make_async_copy(tap, tap_h, sem.at[FIN + 2]))
+    for c in copies:
+        c.start()
+    for i in range(FIN):
+        r = pl.ds(i * rows, rows)
+        out[r, :] = (mine[r, :].astype(F32) + part[r, :].astype(F32)).astype(BF16)
+        copies.append(pltpu.make_async_copy(out.at[r], out_h.at[r], sem.at[i]))
+        copies[-1].start()
+    for c in copies:
+        c.wait()
 
 
 def solution(mesh):
@@ -456,20 +474,24 @@
         ANY = pl.BlockSpec(memory_space=pl.ANY)
         V = pl.BlockSpec(memory_space=pltpu.VMEM)
         rows = 8 * NJ
-        out, cm, tap = pl.pallas_call(
+        HBM = pl.BlockSpec(memory_space=pltpu.HBM)
+        mine, part, cm, tap = pl.pallas_call(
             functools.partial(kernel, n_seq, T, C, D),
             out_shape=(
+                jax.ShapeDtypeStruct((T // 2, D), BF16),
                 jax.ShapeDtypeStruct((T // 2, D), BF16),
                 jax.ShapeDtypeStruct((2, C // n_seq, T * n_seq), BF16),
                 jax.ShapeDtypeStruct((rows, 1, 128), F32),
             ),
-            in_specs=[ANY, ANY, ANY, V, V, ANY],
-            out_specs=(ANY, ANY, V),
+            in_specs=[HBM] * 6,
+            out_specs=(ANY, ANY, ANY, V),
             scratch_shapes=[
+                pltpu.VMEM((NJ, 128), F32),
+                pltpu.VMEM((8 * NJ, 128), F32),
                 pltpu.VMEM((T * 2 * NJ, 128), BF16),
                 pltpu.VMEM((T * 2 * NJ, 128), BF16),
                 pltpu.VMEM((T * NJ, 128), BF16),
-                pltpu.VMEM((D * 2 * NJ, 128), BF16),
+                pltpu.VMEM((WSLOT, D * 2 * NJ // WCH, 128), BF16),
                 pltpu.VMEM((64, 128), BF16),
                 pltpu.VMEM((64, 128), BF16),
                 pltpu.VMEM((T * 2 * NJ, 128), F32),
@@ -477,7 +499,7 @@
                 pltpu.VMEM((T * NJ, 128), F32),
                 pltpu.VMEM((T * NJ, 128), F32),
                 pltpu.VMEM((T + 3, 2, NJ, 128), F32),
-                pltpu.VMEM((UNR, 32 * NJ, 128), F32),
+                pltpu.VMEM((UNR, 2, 128, 128), F32),
                 pltpu.VMEM((2 * NJ, D, 128), BF16),
                 pltpu.VMEM((2, 16 * NJ, 128), F32),
                 pltpu.VMEM((2 * NJ, T, 128), BF16),
@@ -485,19 +507,32 @@
                 pltpu.VMEM((STAGES, 3, NJ, 128), F32),
                 pltpu.VMEM((STAGES, RING, 3, NJ, 128), F32),
                 pltpu.VMEM((T, D), BF16),
-                pltpu.VMEM((T // 2, D), BF16),
-                pltpu.VMEM((T // 2, D), BF16),
                 pltpu.VMEM((rows, 1, 128), F32),
                 pltpu.VMEM((n_seq, 1, 128), F32),
                 pltpu.VMEM((1, 128), F32),
-                dma((3,)), dma((WCH,)), dma((2,)), dma((2,)),
+                dma((5,)), dma((WSLOT,)), dma((2,)), dma((2,)),
                 dma((STAGES, RING)), dma((STAGES, RING)), dma, dma, dma,
                 dma((NT,)), dma((NT,)),
-                dma, dma, dma, dma, dma((NT,)),
+                dma, dma, dma, dma, dma,
             ],
             compiler_params=pltpu.CompilerParams(
-                collective_id=0, has_side_effects=True, vmem_limit_bytes=62 * 1024 * 1024),
-        )(flat(cotangent), flat(conv_input), dec, angle.reshape(NJ, 128), flat(conv_weight), flat(in_weight))
+                collective_id=0, has_side_effects=True, vmem_limit_bytes=46 * 1024 * 1024),
+        )(*[
+                pltpu.with_memory_space_constraint(v, pltpu.HBM)
+                for v in (flat(cotangent), flat(conv_input), dec, angle.reshape(NJ, 128), flat(conv_weight), flat(in_weight))
+            ])
+        out, cm, tap = pl.pallas_call(
+            finish,
+            out_shape=(
+                jax.ShapeDtypeStruct((T // 2, D), BF16),
+                jax.ShapeDtypeStruct(cm.shape, BF16),
+                jax.ShapeDtypeStruct(tap.shape, F32),
+            ),
+            in_specs=[V] * 4,
+            out_specs=(HBM, HBM, HBM),
+            scratch_shapes=[pltpu.VMEM((T // 2, D), BF16), dma((FIN + 3,))],
+            compiler_params=pltpu.CompilerParams(vmem_limit_bytes=16 * 1024 * 1024),
+        )(mine, part, cm, tap)
         tap = tap.reshape(4, NJ, 2, 128).transpose(0, 2, 1, 3).reshape(4, 2, C)
         return out, cm, tap
 

time: 52.7 us -> 39.5 us (0.75)
  Pallas kernels: 45.7 us -> 38.7 us
  local copies, waits for them, and re-layouts: 5.92 us -> 0 us
    pallas_call x1, Pallas kernels: 45.7 us -> 37.3 us  [on_device(): pl.pallas_call(functools.partial(kernel, n_seq, T, C, D), out_shape=(jax....]
    unnamed x3 -> x0, local copies, waits for them, and re-layouts: 5.92 us -> none
    pallas_call x0 -> x1, Pallas kernels: none -> 1.38 us  [on_device(): pl.pallas_call(finish, out_shape=(jax.ShapeDtypeStruct((T // 2, D), BF16)...]
where the time goes in v3:
time: 39.5 us; the launch traced here: 39.4 us
  Pallas kernels  38.7 us (98%)
  between operations  0.64 us (2%)
    pallas_call x1, Pallas kernels, on_device(): pl.pallas_call(functools.partial(kernel, n_seq, T, C, D), out_shape=(jax....  37.3 us
    pallas_call x1, Pallas kernels, on_device(): pl.pallas_call(finish, out_shape=(jax.ShapeDtypeStruct((T // 2, D), BF16)...  1.38 us

profile of v3, /device:TPU:0, one launch (start us, length us, event | category | flops | bytes accessed | tf_op | source)
XLA Modules:
  0.0 39.4 jit_solution(17465326505230437075)
XLA Ops:
  0.6 37.3 %shard_map.85 = (bf16[128,4096]{1,0:T(8,128)(2,1)S(1)}, bf16[128,4096]{1,0:T(8,128)(2,1)S(1)}, bf16[2,16,16384]{2,1,0:T(8,128)(2,1)S(1)}, f32[64,1,128]{2,1,0:T(1,128)S(1)}) custom-call(bf16[4096,128]{1,0:T(8,128)(2,1)} %bitcast.32, bf16[4096,128]{1,0:T(8,128)(2,1)} %bitcast.33, bf16[2048,128]{1,0:T(8,128)(2,1)} %bitcast.34, f32[8,128]{1,0:T(8,128)} %bitcast.36, ...), custom_call_target="tpu_custom_call" | custom-call | tf_op jit(solution)/shard_map/pallas_call | solution.py:478
  38.0 1.4 %shard_map.86 = (bf16[128,4096]{1,0:T(8,128)(2,1)}, bf16[2,16,16384]{2,1,0:T(8,128)(2,1)}, f32[64,1,128]{2,1,0:T(1,128)}) custom-call(bf16[128,4096]{1,0:T(8,128)(2,1)S(1)} %get-tuple-element.10.mine, bf16[128,4096]{1,0:T(8,128)(2,1)S(1)} %get-tuple-element.11.part, bf16[2,16,16384]{2,1,0:T(8,128)(2,1)S(1)} %get-tuple-element.12.cm, ...), custom_call_target="tpu_custom_call" | custom-call | tf_op jit(solution)/shard_map/pallas_call | solution.py:524

commit v4 on v3

--- a/solution.py
+++ b/solution.py
@@ -11,10 +11,12 @@
 F32 = jnp.float32
 BF16 = jnp.bfloat16
 CHUNKS = 8
-WCH = 8
-WSLOT = 4
-W1, W2, W3 = 1, 3, 5
-UNR = 2
+WCH = 2
+WSLOT = 1
+W1, W2, W3, W4 = 0, 1, 1, 2
+H1, H2 = 2, 2
+S2 = 8
+PAD = 64
 FIN = 4
 NT = 8
 RING = 4
@@ -38,8 +40,8 @@
     n_seq, T, C, D,
     cot_h, x_h, dec_h, ang_h, cw_h, w_h,
     mine_h, part_r, cm_h, tap_ref,
-    ang_ref, cw_ref, cot_b, x_b, dec_b, w_b, halo_c, halo_d,
-    cot_f, x_f, e_f, sc_f, g_f, wtmp, wk, ftmp, feat, featT,
+    ang_ref, cw_ref, cot_b, x_b, dec_b, w_b, halo,
+    cot_f, x_f, e_f, sc_f, g_f, seed, sums, perm, wk, ftmp, feat, featT,
     mapv, maps, part, tbuf, trcv, trow,
     in_sem, w_sem, halo_s, halo_r, map_s, map_r, a2a_s, a2a_r, loc_s, par_s, par_r, t1_s, t1_r, t2_s, t2_r, o_sem,
 ):
@@ -62,11 +64,8 @@
     for k in range(STAGES):
         for s in range(1, RING):
             greet(ring(k, s), ch)
-    before, after = lax.rem(me + n_seq - 1, n_seq), lax.rem(me + 1, n_seq)
-    greet(before, ch)
-    greet(after, ch)
     greet(me, other)
-    greetings = STAGES * (RING - 1) + 3
+    greetings = STAGES * (RING - 1) + 1
 
     c_dec = pltpu.make_async_copy(dec_h, dec_b, in_sem.at[0])
     c_cot = pltpu.make_async_copy(cot_h, cot_b, in_sem.at[1])
@@ -148,16 +147,31 @@
         br, bi = br + sr, bi + si
         total = total * st[3 * c + 2]
 
+    raw = dec_b[pl.ds(0, 8 * NJ), :].astype(F32)
+    ftmp[0, pl.ds(0, 8 * NJ), :] = raw
+    halo[0, pl.ds(0, 32), :] = cot_b[pl.ds(0, 32), :]
+    firsts = [ftmp[0, pl.ds(t, NJ, stride=8), :] for t in range(3)]
+    halo[0, pl.ds(32, 32), :] = jnp.concatenate(firsts + firsts[2:], 0).astype(BF16)
     pl.semaphore_wait(barrier, greetings)
 
-    def halo_copies(dst_dev):
-        return [
-            pltpu.make_async_remote_copy(
-                src_ref=s, dst_ref=d, send_sem=halo_s.at[i], recv_sem=halo_r.at[i],
-                device_id=(dst_dev, ch), device_id_type=MESH)
-            for i, (s, d) in enumerate(
-                ((cot_b.at[pl.ds(0, 64)], halo_c), (dec_b.at[pl.ds(0, 64)], halo_d)))
-        ]
+    def halo_copy(k):
+        return pltpu.make_async_remote_copy(
+            src_ref=halo.at[k], dst_ref=halo.at[k + 1], send_sem=halo_s.at[k], recv_sem=halo_r.at[k],
+            device_id=(ring(k, RING - 1), ch), device_id_type=MESH)
+
+    edge = [None]
+    for k in range(1, STAGES):
+        top = place[k - 1] == RING - 1
+        edge.append(top if k == 1 else jnp.logical_and(edge[-1], top))
+
+    def passing(k, act):
+        if k == 0:
+            act(halo_copy(0))
+        else:
+
+            @pl.when(edge[k])
+            def _():
+                act(halo_copy(k))
 
     def map_copy(k, s):
         return pltpu.make_async_remote_copy(
@@ -170,6 +184,9 @@
             maps[k, place[k], i] = v
         for s in range(1, RING):
             map_copy(k, s).start()
+        if k > 0:
+            passing(k - 1, lambda c: c.wait_recv())
+        passing(k, lambda c: c.start())
 
     def stage(k, rot):
         for s in range(1, RING):
@@ -191,53 +208,98 @@
 
     send_map(0, total, br, bi)
 
-    @pl.when(me > 0)
-    def _():
-        for c in halo_copies(before):
-            c.start()
-
-    G = 2 * NJ
+    G = 32 * NJ
+    r, c = (lax.broadcasted_iota(jnp.int32, (G, G), d) for d in range(2))
+    plane, row = r // 16, r % 16
+    perm[...] = (c == row * 2 * NJ + (plane % NJ) * 2 + plane // NJ).astype(F32).astype(BF16)
 
     def unpack_w(i):
         w_copy(i).wait()
-        base = i * (wrows // G)
         src = w_b.at[i % WSLOT]
-
-        def body(k, _):
-            for v in range(UNR):
-                g = k * UNR + v
-                d0 = pl.multiple_of(base + g * 16, 16)
-                for d in range(16):
-                    x = src[pl.ds(pl.multiple_of((g * 16 + d) * G, G), G), :].astype(F32)
-                    for h in range(2):
-                        wtmp[v, h, pl.ds(d * 8, 8), :] = x[h * 8 : h * 8 + 8, :]
-                for p in range(2):
-                    for jt in range(NJ):
-                        x = wtmp[v, jt // 4, pl.ds(2 * (jt % 4) + p, 16, stride=8), :]
-                        wk[p * NJ + jt, pl.ds(d0, 16), :] = x.astype(BF16)
-            return 0
-
-        lax.fori_loop(0, wrows // (G * 16 * UNR), body, 0)
+        n = wrows // G
+        x = jnp.concatenate([src[pl.ds(v * G, G), :] for v in range(n)], 1)
+        y = jnp.dot(perm[...], x, preferred_element_type=F32).astype(BF16)
+        for v in range(n):
+            for q in range(2 * NJ):
+                wk[q, pl.ds((i * n + v) * 16, 16), :] = y[q * 16 : q * 16 + 16, v * 128 : v * 128 + 128]
         if i + WSLOT < WCH:
             w_copy(i + WSLOT).start()
 
     rowwise(dec_b, sc_f, scale_of)
     c_x.wait()
-    rowwise(x_b, x_f, lambda v: v)
+    x_f[pl.ds(0, PAD), :] = jnp.zeros((PAD, 128), F32)
+
+    def spread(i, _):
+        r = pl.multiple_of(i * 64, 64)
+        x_f[pl.ds(PAD + r, 64), :] = x_b[pl.ds(r, 64), :].astype(F32)
+        return 0
+
+    lax.fori_loop(0, x_b.shape[0] // 64, spread, 0)
+
+    b, q = (zero, zero), (one, zero)
+    for c in reversed(range(CHUNKS)):
+        for i, v in enumerate(b + q):
+            seed[c, i] = v
+        ar, ai, sr, si = chunk_maps[c]
+        b = cmul(ar, ai, *b)
+        b = b[0] + sr, b[1] + si
+        q = cmul(ar, ai, *q)
+    for i in range(24):
+        sums[i] = zero
+
+    def split(lo, hi):
+        def two(h, _):
+            def body(n, st):
+                st = list(st)
+                xs = {}
+                for u in reversed(range(8)):
+                    for v in range(2):
+                        t8 = (2 * h + v) * (L // 8) + L // 8 - 1 - n
+                        t = t8 * 8 + u
+                        br, bi, qr, qi = st[4 * v : 4 * v + 4]
+                        a, b = pair(cot_f, t)
+                        br, bi = a + br, b + bi
+                        s = sc_f[at(t8, u), :]
+                        vals = (s * br, s * bi, s * qr, s * qi)
+                        for i, w in enumerate(vals):
+                            g_f[t, i] = w
+                        for k in range(4):
+                            if (v, u - k) not in xs:
+                                xs[v, u - k] = pair(x_f.at[pl.ds(pl.multiple_of(16 * t8 * NJ, 8), PAD + 16 * NJ)], u - k + PAD // (2 * NJ))
+                            xr, xi = xs[v, u - k]
+                            for i, w in enumerate((vals[0] * xr, vals[1] * xi, vals[2] * xr, vals[3] * xr, vals[2] * xi, vals[3] * xi)):
+                                st[8 + 6 * k + i] = st[8 + 6 * k + i] + w
+                        e = e_f[at(t8, u), :]
+                        mr, mi = e * cr, e * ci
+                        st[4 * v : 4 * v + 4] = (*cmul(mr, mi, br, bi), *cmul(mr, mi, qr, qi))
+                return tuple(st)
+
+            st = [seed[2 * h + v, i] for v in range(2) for i in range(4)]
+            st = lax.fori_loop(0, L // 8, body, tuple(st + [sums[i] for i in range(24)]))
+            for i in range(24):
+                sums[i] = st[8 + i]
+            return 0
+
+        lax.fori_loop(lo, hi, two, 0)
+
+    split(0, H1)
     for i in range(0, W1):
         unpack_w(i)
 
     later0, whole0 = stage(0, rot)
     send_map(1, *whole0)
+    split(H1, H2)
     for i in range(W1, W2):
         unpack_w(i)
     rot1 = power(*rot, RING)
     later1, whole1 = stage(1, rot1)
     send_map(2, *whole1)
+    split(H2, CHUNKS // 2)
     for i in range(W2, W3):
         unpack_w(i)
     later2, _ = stage(2, power(*rot1, RING))
 
+    passing(STAGES - 1, lambda c: c.wait_recv())
     ur, ui = later2[2], later2[3]
     for ar, ai, br, bi in (later1, later0):
         ur, ui = cmul(ar, ai, ur, ui)
@@ -247,68 +309,39 @@
 
     @pl.when(jnp.logical_not(last))
     def _():
-        for c in halo_copies(before):
-            c.wait_recv()
-        ftmp[0, pl.ds(0, 64), :] = halo_c[...].astype(F32)
-        ftmp[1, pl.ds(0, 64), :] = halo_d[...].astype(F32)
+        which = 1 + jnp.where(edge[1], 1, 0) + jnp.where(edge[2], 1, 0)
+        rows = halo[which].astype(F32)
+        ftmp[0, pl.ds(0, 64), :] = rows
         vr, vi = ur, ui
         for t in range(3):
-            r = ftmp[1, pl.ds(t, NJ, stride=8), :]
+            r = rows[32 + t * NJ : 32 + (t + 1) * NJ, :]
             e = jnp.exp(r)
             vr, vi = cmul(e * cr, -e * ci, vr, vi)
             s = scale_of(r)
             g_f[T + t, 0] = s * vr
             g_f[T + t, 1] = s * vi
-            a, b = pair(ftmp.at[0], t)
-            vr, vi = vr - a, vi - b
+            g_f[T + t, 2] = zero
+            g_f[T + t, 3] = zero
+            if t < 2:
+                a, b = pair(ftmp.at[0], t)
+                vr, vi = vr - a, vi - b
 
     @pl.when(last)
     def _():
         for t in range(3):
-            g_f[T + t, 0] = zero
-            g_f[T + t, 1] = zero
-
-    init = [None] * CHUNKS
-    for c in reversed(range(CHUNKS)):
-        init[c] = (ur, ui)
-        ar, ai, sr, si = chunk_maps[c]
-        ur, ui = cmul(ar, ai, ur, ui)
-        ur, ui = ur + sr, ui + si
-
-    def pass2(n, st):
-        st = list(st)
-        for u in reversed(range(8)):
-            for c in range(CHUNKS):
-                t8 = c * (L // 8) + L // 8 - 1 - n
-                t = t8 * 8 + u
-                ur, ui = st[2 * c : 2 * c + 2]
-                a, b = pair(cot_f, t)
-                a, b = a + ur, b + ui
-                s = sc_f[at(t8, u), :]
-                g_f[t, 0] = s * a
-                g_f[t, 1] = s * b
-                e = e_f[at(t8, u), :]
-                st[2 * c : 2 * c + 2] = cmul(e * cr, e * ci, a, b)
-        return tuple(st)
-
-    lax.fori_loop(0, L // 8, pass2, tuple(v for u in init for v in u))
-
-    def taps(i, acc):
-        acc = list(acc)
-        for p in range(2):
-            g = [g_f[i * 8 + k, p] for k in range(3)]
-            for u in range(8):
-                g.append(g_f[i * 8 + u + 3, p])
-                x = x_f[pl.ds(2 * NJ * (i * 8 + u) + p, NJ, stride=2), :]
-                for k in range(4):
-                    acc[2 * k + p] = acc[2 * k + p] + g[u + k] * x
-        return tuple(acc)
-
-    acc = lax.fori_loop(0, T // 8, taps, (zero,) * 8)
+            for i in range(4):
+                g_f[T + t, i] = zero
+
     for k in range(4):
+        a = [sums[6 * k + i] for i in range(6)]
+        acc = [a[0] + a[2] * ur - a[3] * ui, a[1] + a[4] * ui + a[5] * ur]
+        for t in range(k):
+            x = pair(x_f, T + t - k + PAD // (2 * NJ))
+            for p in range(2):
+                acc[p] = acc[p] + g_f[T + t, p] * x[p]
         for p in range(2):
             for jt in range(NJ):
-                tbuf[2 * NJ * k + 2 * jt + p] = acc[2 * k + p][jt : jt + 1, :]
+                tbuf[2 * NJ * k + 2 * jt + p] = acc[p][jt : jt + 1, :]
     trcv[me] = tbuf[me]
 
     def t1(dst_dev):
@@ -335,10 +368,14 @@
     cw = [[cw_ref[pl.ds(2 * NJ * k + p, NJ, stride=2), :] for p in range(2)] for k in range(4)]
 
     def conv(i, _):
+        def full(t):
+            hr, hi = cmul(g_f[t, 2], g_f[t, 3], ur, ui)
+            return g_f[t, 0] + hr, g_f[t, 1] + hi
+
+        both = [full(i * 16 + k) for k in range(19)]
         for p in range(2):
-            g = [g_f[i * 16 + k, p] for k in range(3)]
+            g = [v[p] for v in both]
             for u in range(16):
-                g.append(g_f[i * 16 + u + 3, p])
                 f = cw[0][p] * g[u] + cw[1][p] * g[u + 1] + cw[2][p] * g[u + 2] + cw[3][p] * g[u + 3]
                 ftmp[p, pl.ds((u // 8) * 8 * NJ + u % 8, NJ, stride=8), :] = f
             for jt in range(NJ):
@@ -377,11 +414,26 @@
 
         return 0
 
-    lax.fori_loop(0, NJ, turn, 0)
+    lax.fori_loop(0, S2, turn, 0)
+
+    for i in range(W3, W4):
+        unpack_w(i)
+
+    def all_but_one(ref, sem):
+        part_of = ref.at[pl.ds(0, n_seq - 1)]
+        return pltpu.make_async_copy(part_of, part_of, sem)
+
+    all_but_one(trcv, t1_r).wait()
+    row = jnp.sum(trcv[...], axis=0)
+    trow[...] = row
+    tap_ref[me] = row
+    others(lambda j: t2(j).start())
+
+    for i in range(W4, WCH):
+        unpack_w(i)
+
+    lax.fori_loop(S2, NJ, turn, 0)
     local.start()
-
-    for i in range(W3, WCH):
-        unpack_w(i)
 
     nt = D // NT
     half = T // 2
@@ -401,19 +453,8 @@
         par_copy(n).start()
         return 0
 
-    lax.fori_loop(0, NT // 2, tile, 0)
-
-    def all_but_one(ref, sem):
-        part_of = ref.at[pl.ds(0, n_seq - 1)]
-        return pltpu.make_async_copy(part_of, part_of, sem)
-
-    all_but_one(trcv, t1_r).wait()
-    row = jnp.sum(trcv[...], axis=0)
-    trow[...] = row
-    tap_ref[me] = row
-    others(lambda j: t2(j).start())
-
-    lax.fori_loop(NT // 2, NT, tile, 0)
+    lax.fori_loop(0, NT, tile, 0)
+
 
     mine = pltpu.make_async_copy(part.at[pl.ds(pl.multiple_of(ch * half, half), half), :], mine_h, o_sem)
     mine.start()
@@ -422,10 +463,8 @@
         for s in range(1, RING):
             map_copy(k, s).wait_send()
 
-    @pl.when(me > 0)
-    def _():
-        for c in halo_copies(before):
-            c.wait_send()
+    for k in range(STAGES):
+        passing(k, lambda c: c.wait_send())
 
     def ends(n, _):
         par_copy(n).wait()
@@ -492,14 +531,15 @@
                 pltpu.VMEM((T * 2 * NJ, 128), BF16),
                 pltpu.VMEM((T * NJ, 128), BF16),
                 pltpu.VMEM((WSLOT, D * 2 * NJ // WCH, 128), BF16),
-                pltpu.VMEM((64, 128), BF16),
-                pltpu.VMEM((64, 128), BF16),
+                pltpu.VMEM((STAGES + 1, 64, 128), BF16),
                 pltpu.VMEM((T * 2 * NJ, 128), F32),
-                pltpu.VMEM((T * 2 * NJ, 128), F32),
+                pltpu.VMEM((T * 2 * NJ + PAD, 128), F32),
                 pltpu.VMEM((T * NJ, 128), F32),
                 pltpu.VMEM((T * NJ, 128), F32),
-                pltpu.VMEM((T + 3, 2, NJ, 128), F32),
-                pltpu.VMEM((UNR, 2, 128, 128), F32),
+                pltpu.VMEM((T + 3, 4, NJ, 128), F32),
+                pltpu.VMEM((CHUNKS, 4, NJ, 128), F32),
+                pltpu.VMEM((24, NJ, 128), F32),
+                pltpu.VMEM((32 * NJ, 32 * NJ), BF16),
                 pltpu.VMEM((2 * NJ, D, 128), BF16),
                 pltpu.VMEM((2, 16 * NJ, 128), F32),
                 pltpu.VMEM((2 * NJ, T, 128), BF16),
@@ -510,7 +550,7 @@
                 pltpu.VMEM((rows, 1, 128), F32),
                 pltpu.VMEM((n_seq, 1, 128), F32),
                 pltpu.VMEM((1, 128), F32),
-                dma((5,)), dma((WSLOT,)), dma((2,)), dma((2,)),
+                dma((5,)), dma((WSLOT,)), dma((STAGES,)), dma((STAGES,)),
                 dma((STAGES, RING)), dma((STAGES, RING)), dma, dma, dma,
                 dma((NT,)), dma((NT,)),
                 dma, dma, dma, dma, dma,

time: 39.5 us -> 37.2 us (0.942)
  Pallas kernels: 38.7 us -> 36.5 us
    pallas_call x1, Pallas kernels: 37.3 us -> 35.1 us  [on_device(): pl.pallas_call(functools.partial(kernel, n_seq, T, C, D), out_shape=(jax....]
where the time goes in v4:
time: 37.2 us; the launch traced here: 37.1 us
  Pallas kernels  36.5 us (98%)
  between operations  0.64 us (2%)
    pallas_call x1, Pallas kernels, on_device(): pl.pallas_call(functools.partial(kernel, n_seq, T, C, D), out_shape=(jax....  35.1 us
    pallas_call x1, Pallas kernels, on_device(): pl.pallas_call(finish, out_shape=(jax.ShapeDtypeStruct((T // 2, D), BF16)...  1.38 us

profile of v4, /device:TPU:0, one launch (start us, length us, event | category | flops | bytes accessed | tf_op | source)
XLA Modules:
  0.0 37.1 jit_solution(296484593449704933)
XLA Ops:
  0.6 35.1 %shard_map.85 = (bf16[128,4096]{1,0:T(8,128)(2,1)S(1)}, bf16[128,4096]{1,0:T(8,128)(2,1)S(1)}, bf16[2,16,16384]{2,1,0:T(8,128)(2,1)S(1)}, f32[64,1,128]{2,1,0:T(1,128)S(1)}) custom-call(bf16[4096,128]{1,0:T(8,128)(2,1)} %bitcast.32, bf16[4096,128]{1,0:T(8,128)(2,1)} %bitcast.33, bf16[2048,128]{1,0:T(8,128)(2,1)} %bitcast.34, f32[8,128]{1,0:T(8,128)} %bitcast.36, ...), custom_call_target="tpu_custom_call" | custom-call | tf_op jit(solution)/shard_map/pallas_call | solution.py:517
  35.7 1.4 %shard_map.86 = (bf16[128,4096]{1,0:T(8,128)(2,1)}, bf16[2,16,16384]{2,1,0:T(8,128)(2,1)}, f32[64,1,128]{2,1,0:T(1,128)}) custom-call(bf16[128,4096]{1,0:T(8,128)(2,1)S(1)} %get-tuple-element.10.mine, bf16[128,4096]{1,0:T(8,128)(2,1)S(1)} %get-tuple-element.11.part, bf16[2,16,16384]{2,1,0:T(8,128)(2,1)S(1)} %get-tuple-element.12.cm, ...), custom_call_target="tpu_custom_call" | custom-call | tf_op jit(solution)/shard_map/pallas_call | solution.py:564

commit v5 on v4

--- a/solution.py
+++ b/solution.py
@@ -15,7 +15,7 @@
 WSLOT = 1
 W1, W2, W3, W4 = 0, 1, 1, 2
 H1, H2 = 2, 2
-S2 = 8
+S2 = 6
 PAD = 64
 FIN = 4
 NT = 8
@@ -444,6 +444,11 @@
             src_ref=part.at[pl.ds(pl.multiple_of(other * half, half), half), cols], dst_ref=part_r.at[:, cols],
             send_sem=par_s.at[n], recv_sem=par_r.at[n], device_id=(me, other), device_id_type=MESH)
 
+    def mine_copy(n):
+        cols = pl.ds(pl.multiple_of(n * nt, nt), nt)
+        return pltpu.make_async_copy(
+            part.at[pl.ds(pl.multiple_of(ch * half, half), half), cols], mine_h.at[:, cols], o_sem.at[n])
+
     def tile(n, _):
         rows = pl.ds(pl.multiple_of(n * nt, nt), nt)
         lhs = jnp.concatenate([feat[i] for i in range(2 * NJ)], 1)
@@ -451,13 +456,11 @@
         y = lax.dot_general(lhs, rhs, (((1,), (1,)), ((), ())), preferred_element_type=F32)
         part[:, rows] = y.astype(BF16)
         par_copy(n).start()
+        mine_copy(n).start()
         return 0
 
     lax.fori_loop(0, NT, tile, 0)
 
-
-    mine = pltpu.make_async_copy(part.at[pl.ds(pl.multiple_of(ch * half, half), half), :], mine_h, o_sem)
-    mine.start()
 
     for k in range(STAGES):
         for s in range(1, RING):
@@ -468,10 +471,10 @@
 
     def ends(n, _):
         par_copy(n).wait()
+        mine_copy(n).wait()
         return 0
 
     lax.fori_loop(0, NT, ends, 0)
-    mine.wait()
     all_but_one(trcv, t1_s).wait()
     all_but_one(trcv, t2_s).wait()
     all_but_one(tap_ref, t2_r).wait()
@@ -553,7 +556,7 @@
                 dma((5,)), dma((WSLOT,)), dma((STAGES,)), dma((STAGES,)),
                 dma((STAGES, RING)), dma((STAGES, RING)), dma, dma, dma,
                 dma((NT,)), dma((NT,)),
-                dma, dma, dma, dma, dma,
+                dma, dma, dma, dma, dma((NT,)),
             ],
             compiler_params=pltpu.CompilerParams(
                 collective_id=0, has_side_effects=True, vmem_limit_bytes=46 * 1024 * 1024),

time: 37.2 us -> 36.6 us (0.984)
  Pallas kernels: 36.5 us -> 35.9 us
    pallas_call x1, Pallas kernels: 35.1 us -> 34.5 us  [on_device(): pl.pallas_call(functools.partial(kernel, n_seq, T, C, D), out_shape=(jax....]
where the time goes in v5:
time: 36.6 us; the launch traced here: 36.5 us
  Pallas kernels  35.9 us (98%)
  between operations  0.64 us (2%)
    pallas_call x1, Pallas kernels, on_device(): pl.pallas_call(functools.partial(kernel, n_seq, T, C, D), out_shape=(jax....  34.5 us
    pallas_call x1, Pallas kernels, on_device(): pl.pallas_call(finish, out_shape=(jax.ShapeDtypeStruct((T // 2, D), BF16)...  1.38 us

profile of v5, /device:TPU:0, one launch (start us, length us, event | category | flops | bytes accessed | tf_op | source)
XLA Modules:
  0.0 36.5 jit_solution(10809555576475044151)
XLA Ops:
  0.6 34.5 %shard_map.85 = (bf16[128,4096]{1,0:T(8,128)(2,1)S(1)}, bf16[128,4096]{1,0:T(8,128)(2,1)S(1)}, bf16[2,16,16384]{2,1,0:T(8,128)(2,1)S(1)}, f32[64,1,128]{2,1,0:T(1,128)S(1)}) custom-call(bf16[4096,128]{1,0:T(8,128)(2,1)} %bitcast.32, bf16[4096,128]{1,0:T(8,128)(2,1)} %bitcast.33, bf16[2048,128]{1,0:T(8,128)(2,1)} %bitcast.34, f32[8,128]{1,0:T(8,128)} %bitcast.36, ...), custom_call_target="tpu_custom_call" | custom-call | tf_op jit(solution)/shard_map/pallas_call | solution.py:520
  35.1 1.4 %shard_map.86 = (bf16[128,4096]{1,0:T(8,128)(2,1)}, bf16[2,16,16384]{2,1,0:T(8,128)(2,1)}, f32[64,1,128]{2,1,0:T(1,128)}) custom-call(bf16[128,4096]{1,0:T(8,128)(2,1)S(1)} %get-tuple-element.10.mine, bf16[128,4096]{1,0:T(8,128)(2,1)S(1)} %get-tuple-element.11.part, bf16[2,16,16384]{2,1,0:T(8,128)(2,1)S(1)} %get-tuple-element.12.cm, ...), custom_call_target="tpu_custom_call" | custom-call | tf_op jit(solution)/shard_map/pallas_call | solution.py:567
